TPU v7x, 32 devices: a whole 2x2x4 slice. The times are simulated.
32 devices in a mesh: fsdp: 4 (over y, x), ctx: 4 (over z), tp: 2 (over core).
Axes of the slice: x: 2, y: 2, z: 4, core: 2. Of those that a mesh axis runs over, the one named last changes fastest.
Arguments:
- inputs: bfloat16 [4, 2048, 1024], P('fsdp', 'ctx'), may hold values from -6 to 6
- encoder_states: bfloat16 [4, 256, 1024], P('fsdp', 'ctx'), may hold values from -6 to 6
- seq_lengths: int32 [4], P('fsdp'), may hold values from 512 to 2048, as said below
- enc_lengths: int32 [4], P('fsdp'), may hold values from 64 to 256, as said below
- cotangent: bfloat16 [4, 2048, 1024], P('fsdp', 'ctx'), may hold values from -6 to 6
- norm_gains: bfloat16 [4, 1024], P(None, ('fsdp', 'ctx')), may hold values from 0.5 to 1.5
- norm_biases: bfloat16 [4, 1024], P(None, ('fsdp', 'ctx')), may hold values from -3 to 3
- w_query: bfloat16 [1024, 1024], P(('fsdp', 'ctx'), 'tp'), may hold values from -0.1875 to 0.1875
- w_key: bfloat16 [1024, 1024], P(('fsdp', 'ctx'), 'tp'), may hold values from -0.1875 to 0.1875
- w_value: bfloat16 [1024, 1024], P(('fsdp', 'ctx'), 'tp'), may hold values from -0.1875 to 0.1875
- w_out: bfloat16 [1024, 1024], P('tp', ('fsdp', 'ctx')), may hold values from -1.5 to 1.5
- w_cross_query: bfloat16 [1024, 1024], P(('fsdp', 'ctx'), 'tp'), may hold values from -0.1875 to 0.1875
- w_cross_key: bfloat16 [1024, 1024], P(('fsdp', 'ctx'), 'tp'), may hold values from -0.1875 to 0.1875
- w_cross_value: bfloat16 [1024, 1024], P(('fsdp', 'ctx'), 'tp'), may hold values from -0.1875 to 0.1875
- w_cross_out: bfloat16 [1024, 1024], P('tp', ('fsdp', 'ctx')), may hold values from -1 to 1
- w_inner: bfloat16 [1024, 4096], P(('fsdp', 'ctx'), 'tp'), may hold values from -0.1875 to 0.1875
- w_outer: bfloat16 [4096, 1024], P('tp', ('fsdp', 'ctx')), may hold values from -0.125 to 0.125
Outputs:
- output: float32 [4, 2048, 1024], P('fsdp', 'ctx')
- input_grad: float32 [4, 2048, 1024], P('fsdp', 'ctx')
- encoder_grad: float32 [4, 256, 1024], P('fsdp', 'ctx')
- grad_norm_gains: float32 [4, 1024], P(None, ('fsdp', 'ctx'))
- grad_norm_biases: float32 [4, 1024], P(None, ('fsdp', 'ctx'))
- grad_query: float32 [1024, 1024], P(('fsdp', 'ctx'), 'tp')
- grad_key: float32 [1024, 1024], P(('fsdp', 'ctx'), 'tp')
- grad_value: float32 [1024, 1024], P(('fsdp', 'ctx'), 'tp')
- grad_out: float32 [1024, 1024], P('tp', ('fsdp', 'ctx'))
- grad_cross_query: float32 [1024, 1024], P(('fsdp', 'ctx'), 'tp')
- grad_cross_key: float32 [1024, 1024], P(('fsdp', 'ctx'), 'tp')
- grad_cross_value: float32 [1024, 1024], P(('fsdp', 'ctx'), 'tp')
- grad_cross_out: float32 [1024, 1024], P('tp', ('fsdp', 'ctx'))
- grad_inner: float32 [1024, 4096], P(('fsdp', 'ctx'), 'tp')
- grad_outer: float32 [4096, 1024], P('tp', ('fsdp', 'ctx'))
Inputs may be any that keep to these rules, and one draw needn't show every extreme that they name: `seq_lengths`: each sequence's valid slots are its first ones; some sequence has exactly 2048 and some exactly 512. `enc_lengths`: each sequence's valid encoder rows are its first ones; some sequence has exactly 256 and some exactly 64.
All inputs are finite; a program needn't handle non-finite values.
Results may differ from a plain program's by a relative error of at most 0.018.
Values may be sent and summed in bfloat16 or wider, within the bound.
No kernel may reach another device: no remote copies, remote signals or barrier semaphores. Data moves between devices by JAX's collectives and lax.ppermute only.
A program may use at most 192 MiB of HBM per device.

v0:
```python
import jax
import jax.numpy as jnp
from jax import lax
from jax.sharding import PartitionSpec as P

HEAD_DIM = 64


EPS = 1e-05


def smooth_gate(values):
    return (
        0.5
        * values
        * (1.0 + jnp.tanh(0.7978845608028654 * (values + 0.044715 * values * values * values)))
    )


def fetch_weights(shards):
    return (
        lax.all_gather(shards[0], ("fsdp", "ctx"), axis=1, tiled=True),
        lax.all_gather(shards[1], ("fsdp", "ctx"), axis=1, tiled=True),
        lax.all_gather(shards[2], ("fsdp", "ctx"), axis=0, tiled=True),
        lax.all_gather(shards[3], ("fsdp", "ctx"), axis=0, tiled=True),
        lax.all_gather(shards[4], ("fsdp", "ctx"), axis=0, tiled=True),
        lax.all_gather(shards[5], ("fsdp", "ctx"), axis=1, tiled=True),
        lax.all_gather(shards[6], ("fsdp", "ctx"), axis=0, tiled=True),
        lax.all_gather(shards[7], ("fsdp", "ctx"), axis=0, tiled=True),
        lax.all_gather(shards[8], ("fsdp", "ctx"), axis=0, tiled=True),
        lax.all_gather(shards[9], ("fsdp", "ctx"), axis=1, tiled=True),
        lax.all_gather(shards[10], ("fsdp", "ctx"), axis=0, tiled=True),
        lax.all_gather(shards[11], ("fsdp", "ctx"), axis=1, tiled=True),
    )


def return_grads(grads):
    return tuple(
        (
            lax.psum_scatter(grads[0], ("fsdp", "ctx"), scatter_dimension=1, tiled=True),
            lax.psum_scatter(grads[1], ("fsdp", "ctx"), scatter_dimension=1, tiled=True),
            lax.psum_scatter(grads[2], ("fsdp", "ctx"), scatter_dimension=0, tiled=True),
            lax.psum_scatter(grads[3], ("fsdp", "ctx"), scatter_dimension=0, tiled=True),
            lax.psum_scatter(grads[4], ("fsdp", "ctx"), scatter_dimension=0, tiled=True),
            lax.psum_scatter(grads[5], ("fsdp", "ctx"), scatter_dimension=1, tiled=True),
            lax.psum_scatter(grads[6], ("fsdp", "ctx"), scatter_dimension=0, tiled=True),
            lax.psum_scatter(grads[7], ("fsdp", "ctx"), scatter_dimension=0, tiled=True),
            lax.psum_scatter(grads[8], ("fsdp", "ctx"), scatter_dimension=0, tiled=True),
            lax.psum_scatter(grads[9], ("fsdp", "ctx"), scatter_dimension=1, tiled=True),
            lax.psum_scatter(grads[10], ("fsdp", "ctx"), scatter_dimension=0, tiled=True),
            lax.psum_scatter(grads[11], ("fsdp", "ctx"), scatter_dimension=1, tiled=True),
        )
    )


def head_total(partial_sum):
    return lax.psum(partial_sum, "tp")


def input_total(partial_sum):
    return lax.psum(partial_sum, "tp")


def key_totals(grad_keys, grad_values):
    return (
        lax.psum_scatter(grad_keys, "ctx", scatter_dimension=0, tiled=True),
        lax.psum_scatter(grad_values, "ctx", scatter_dimension=0, tiled=True),
    )


def mult(left, right):
    return jnp.dot(left, right, preferred_element_type=jnp.float32)


def mult_t(left, right):
    return lax.dot_general(
        left, right, (((0,), (0,)), ((), ())), preferred_element_type=jnp.float32
    )


def mult_nt(left, right):
    return lax.dot_general(
        left, right, (((1,), (1,)), ((), ())), preferred_element_type=jnp.float32
    )


def by_heads(matrix):
    return matrix.reshape(matrix.shape[0], matrix.shape[1] // HEAD_DIM, HEAD_DIM)


def norm_parts(values):
    mean = jnp.mean(values, axis=-1, keepdims=True)
    centred = values - mean
    scale = lax.rsqrt(jnp.mean(centred * centred, axis=-1, keepdims=True) + EPS)
    return (centred * scale, scale)


def norm_back(grad_result, normed, scale, gain):
    grad_normed = grad_result * gain
    grad_input = scale * (
        grad_normed
        - jnp.mean(grad_normed, axis=-1, keepdims=True)
        - normed * jnp.mean(grad_normed * normed, axis=-1, keepdims=True)
    )
    return (grad_input, jnp.sum(grad_result * normed, axis=0), jnp.sum(grad_result, axis=0))


def block_scores(query, keys, positions, start, limit, causal):
    score = jnp.einsum(
        "qhe,khe->hqk", query, keys, preferred_element_type=jnp.float32
    ) * HEAD_DIM ** (-0.5)
    key_places = start + lax.iota(jnp.int32, keys.shape[0])
    allowed = key_places[None, :] < limit
    if causal:
        allowed = allowed & (key_places[None, :] <= positions[:, None])
    return (score, allowed[None])


def sweep(members, kblock, update, carry):
    count = members[0].shape[0] // kblock

    def step(block_index, state):
        start = block_index * kblock
        pieces = tuple((lax.dynamic_slice_in_dim(member, start, kblock, 0) for member in members))
        return update(state, pieces, start)

    return lax.fori_loop(0, count, step, carry)


def attend(query, keys, values, positions, limit, causal):
    rows, heads, depth = query.shape
    qblock = min(512, rows)
    kblock = min(512, keys.shape[0])

    def one_block(item):
        query_part, place_part = item

        def stats(state, pieces, start):
            top, total = state
            score, allowed = block_scores(query_part, pieces[0], place_part, start, limit, causal)
            score = jnp.where(allowed, score, -1e30)
            new_top = jnp.maximum(top, jnp.max(score, axis=-1))
            weights = jnp.where(allowed, jnp.exp(score - new_top[..., None]), 0.0)
            return (new_top, total * jnp.exp(top - new_top) + jnp.sum(weights, axis=-1))

        begin = (
            jnp.full((heads, qblock), -1e30, jnp.float32),
            jnp.zeros((heads, qblock), jnp.float32),
        )
        top, total = sweep((keys,), kblock, stats, begin)
        log_total = top + jnp.log(total)

        def collect(acc, pieces, start):
            score, allowed = block_scores(query_part, pieces[0], place_part, start, limit, causal)
            chance = jnp.where(allowed, jnp.exp(score - log_total[..., None]), 0.0).astype(
                jnp.bfloat16
            )
            return acc + jnp.einsum(
                "hqk,khe->qhe", chance, pieces[1], preferred_element_type=jnp.float32
            )

        mixed = sweep(
            (keys, values), kblock, collect, jnp.zeros((qblock, heads, depth), jnp.float32)
        )
        return (mixed, log_total)

    mixed_all, log_totals = lax.map(
        one_block,
        (
            query.reshape(rows // qblock, qblock, heads, depth),
            positions.reshape(rows // qblock, qblock),
        ),
    )
    return (mixed_all.reshape(rows, heads * depth), log_totals)


def attend_back(query, keys, values, grad_mixed, log_totals, positions, limit, causal):
    rows, heads, depth = query.shape
    qblock = min(512, rows)
    kblock = min(512, keys.shape[0])

    def one_block(carry, item):
        query_part, grad_part, total_part, place_part = item

        def block_probs(pieces, start):
            score, allowed = block_scores(query_part, pieces[0], place_part, start, limit, causal)
            chance = jnp.where(allowed, jnp.exp(score - total_part[..., None]), 0.0)
            slopes = jnp.einsum(
                "qhe,khe->hqk", grad_part, pieces[1], preferred_element_type=jnp.float32
            )
            return (chance, slopes)

        def accumulate(state, pieces, start):
            chance, slopes = block_probs(pieces, start)
            return state + jnp.sum(chance * slopes, axis=-1)

        delta = sweep((keys, values), kblock, accumulate, jnp.zeros((heads, qblock), jnp.float32))

        def backward_step(state, pieces, start):
            grad_query, grad_keys, grad_values = state
            chance, slopes = block_probs(pieces, start)
            grad_scores = (chance * (slopes - delta[..., None])).astype(jnp.bfloat16)
            grad_query = grad_query + HEAD_DIM ** (-0.5) * jnp.einsum(
                "hqk,khe->qhe", grad_scores, pieces[0], preferred_element_type=jnp.float32
            )
            key_part = HEAD_DIM ** (-0.5) * jnp.einsum(
                "hqk,qhe->khe", grad_scores, query_part, preferred_element_type=jnp.float32
            )
            value_part = jnp.einsum(
                "hqk,qhe->khe",
                chance.astype(jnp.bfloat16),
                grad_part,
                preferred_element_type=jnp.float32,
            )
            grad_keys = lax.dynamic_update_slice_in_dim(
                grad_keys,
                lax.dynamic_slice_in_dim(grad_keys, start, kblock, 0) + key_part,
                start,
                0,
            )
            grad_values = lax.dynamic_update_slice_in_dim(
                grad_values,
                lax.dynamic_slice_in_dim(grad_values, start, kblock, 0) + value_part,
                start,
                0,
            )
            return (grad_query, grad_keys, grad_values)

        grad_query, grad_keys, grad_values = sweep(
            (keys, values),
            kblock,
            backward_step,
            (jnp.zeros((qblock, heads, depth), jnp.float32), carry[0], carry[1]),
        )
        return ((grad_keys, grad_values), grad_query)

    empty = jnp.zeros(keys.shape, jnp.float32)
    (grad_keys, grad_values), grad_queries = lax.scan(
        one_block,
        (empty, empty),
        (
            query.reshape(rows // qblock, qblock, heads, depth),
            grad_mixed.reshape(rows // qblock, qblock, heads, depth),
            log_totals,
            positions.reshape(rows // qblock, qblock),
        ),
    )
    return (
        grad_queries.reshape(rows, heads * depth),
        grad_keys.reshape(keys.shape[0], heads * depth),
        grad_values.reshape(keys.shape[0], heads * depth),
    )


def body(
    inputs,
    encoder_states,
    seq_lengths,
    enc_lengths,
    cotangent,
    norm_gains,
    norm_biases,
    w_query,
    w_key,
    w_value,
    w_out,
    w_cross_query,
    w_cross_key,
    w_cross_value,
    w_cross_out,
    w_inner,
    w_outer,
):
    gathered = fetch_weights(
        (
            norm_gains,
            norm_biases,
            w_query,
            w_key,
            w_value,
            w_out,
            w_cross_query,
            w_cross_key,
            w_cross_value,
            w_cross_out,
            w_inner,
            w_outer,
        )
    )
    gains = gathered[0].astype(jnp.float32)
    biases = gathered[1].astype(jnp.float32)
    full_query, full_key, full_value, full_out = (
        gathered[2],
        gathered[3],
        gathered[4],
        gathered[5],
    )
    cross_query_w, cross_key_w, cross_value_w, cross_out_w = (
        gathered[6],
        gathered[7],
        gathered[8],
        gathered[9],
    )
    full_inner, full_outer = (gathered[10], gathered[11])
    rows = inputs.shape[1]
    hidden_x = inputs[0].astype(jnp.float32)
    enc_rows = encoder_states[0]
    seq_limit = seq_lengths[0]
    enc_limit = enc_lengths[0]
    positions = lax.axis_index("ctx") * rows + lax.iota(jnp.int32, rows)
    valid = (positions < seq_limit).astype(jnp.float32)[:, None]
    normed_a, scale_a = norm_parts(hidden_x)
    attn_in = (normed_a * gains[0] + biases[0]).astype(jnp.bfloat16)
    query = mult(attn_in, full_query).astype(jnp.bfloat16)
    keys_own = mult(attn_in, full_key).astype(jnp.bfloat16)
    values_own = mult(attn_in, full_value).astype(jnp.bfloat16)
    cross_keys_own = mult(enc_rows, cross_key_w).astype(jnp.bfloat16)
    cross_values_own = mult(enc_rows, cross_value_w).astype(jnp.bfloat16)
    keys_all, values_all, cross_keys, cross_values = (
        lax.all_gather(keys_own, "ctx", axis=0, tiled=True),
        lax.all_gather(values_own, "ctx", axis=0, tiled=True),
        lax.all_gather(cross_keys_own, "ctx", axis=0, tiled=True),
        lax.all_gather(cross_values_own, "ctx", axis=0, tiled=True),
    )
    attn_mixed, attn_totals = attend(
        by_heads(query), by_heads(keys_all), by_heads(values_all), positions, seq_limit, True
    )
    attn_flat = attn_mixed.astype(jnp.bfloat16)
    first = hidden_x + head_total(mult(attn_flat, full_out))
    normed_c, scale_c = norm_parts(first)
    cross_in = (normed_c * gains[1] + biases[1]).astype(jnp.bfloat16)
    cross_query = mult(cross_in, cross_query_w).astype(jnp.bfloat16)
    cross_mixed, cross_totals = attend(
        by_heads(cross_query),
        by_heads(cross_keys),
        by_heads(cross_values),
        positions,
        enc_limit,
        False,
    )
    cross_flat = cross_mixed.astype(jnp.bfloat16)
    second = first + head_total(mult(cross_flat, cross_out_w))
    normed_f, scale_f = norm_parts(second)
    ffn_in = (normed_f * gains[2] + biases[2]).astype(jnp.bfloat16)
    inner = mult(ffn_in, full_inner)
    gated, gate_pullback = jax.vjp(smooth_gate, inner)
    active = gated.astype(jnp.bfloat16)
    third = second + head_total(mult(active, full_outer))
    normed_y, scale_y = norm_parts(third)
    output = (normed_y * gains[3] + biases[3]) * valid
    grad_y = cotangent[0].astype(jnp.float32) * valid
    grad_third, gain_y, bias_y = norm_back(grad_y, normed_y, scale_y, gains[3])
    grad_third_low = grad_third.astype(jnp.bfloat16)
    grad_w_outer = mult_t(active, grad_third_low)
    grad_active = mult_nt(grad_third_low, full_outer)
    grad_active_low = gate_pullback(grad_active)[0].astype(jnp.bfloat16)
    grad_w_inner = mult_t(ffn_in, grad_active_low)
    grad_ffn_in = input_total(mult_nt(grad_active_low, full_inner))
    grad_second_part, gain_f, bias_f = norm_back(grad_ffn_in, normed_f, scale_f, gains[2])
    grad_second = grad_third + grad_second_part
    grad_second_low = grad_second.astype(jnp.bfloat16)
    grad_w_cross_out = mult_t(cross_flat, grad_second_low)
    grad_cross_low = mult_nt(grad_second_low, cross_out_w).astype(jnp.bfloat16)
    cross_gq, cross_gk, cross_gv = attend_back(
        by_heads(cross_query),
        by_heads(cross_keys),
        by_heads(cross_values),
        by_heads(grad_cross_low),
        cross_totals,
        positions,
        enc_limit,
        False,
    )
    own_ck, own_cv = key_totals(cross_gk, cross_gv)
    grad_cq = cross_gq.astype(jnp.bfloat16)
    grad_ck = own_ck.astype(jnp.bfloat16)
    grad_cv = own_cv.astype(jnp.bfloat16)
    grad_w_cross_query = mult_t(cross_in, grad_cq)
    grad_w_cross_key = mult_t(enc_rows, grad_ck)
    grad_w_cross_value = mult_t(enc_rows, grad_cv)
    grad_cross_in, grad_encoder = lax.psum(
        (
            mult_nt(grad_cq, cross_query_w),
            mult_nt(grad_ck, cross_key_w) + mult_nt(grad_cv, cross_value_w),
        ),
        "tp",
    )
    grad_first_part, gain_c, bias_c = norm_back(grad_cross_in, normed_c, scale_c, gains[1])
    grad_first = grad_second + grad_first_part
    grad_first_low = grad_first.astype(jnp.bfloat16)
    grad_w_out = mult_t(attn_flat, grad_first_low)
    grad_attn_low = mult_nt(grad_first_low, full_out).astype(jnp.bfloat16)
    self_gq, self_gk, self_gv = attend_back(
        by_heads(query),
        by_heads(keys_all),
        by_heads(values_all),
        by_heads(grad_attn_low),
        attn_totals,
        positions,
        seq_limit,
        True,
    )
    own_k, own_v = key_totals(self_gk, self_gv)
    grad_q = self_gq.astype(jnp.bfloat16)
    grad_k = own_k.astype(jnp.bfloat16)
    grad_v = own_v.astype(jnp.bfloat16)
    grad_w_query = mult_t(attn_in, grad_q)
    grad_w_key = mult_t(attn_in, grad_k)
    grad_w_value = mult_t(attn_in, grad_v)
    grad_attn_in = input_total(
        mult_nt(grad_q, full_query) + mult_nt(grad_k, full_key) + mult_nt(grad_v, full_value)
    )
    grad_x_part, gain_a, bias_a = norm_back(grad_attn_in, normed_a, scale_a, gains[0])
    grad_inputs = grad_first + grad_x_part
    grad_gains = jnp.stack([gain_a, gain_c, gain_f, gain_y])
    grad_biases = jnp.stack([bias_a, bias_c, bias_f, bias_y])
    shares = return_grads(
        (
            grad_gains,
            grad_biases,
            grad_w_query,
            grad_w_key,
            grad_w_value,
            grad_w_out,
            grad_w_cross_query,
            grad_w_cross_key,
            grad_w_cross_value,
            grad_w_cross_out,
            grad_w_inner,
            grad_w_outer,
        )
    )
    return (output[None], grad_inputs[None], grad_encoder[None]) + tuple(shares)


def solution(mesh):
    placed = (
        P("fsdp", "ctx", None),
        P("fsdp", "ctx", None),
        P("fsdp"),
        P("fsdp"),
        P("fsdp", "ctx", None),
        P(None, ("fsdp", "ctx")),
        P(None, ("fsdp", "ctx")),
        P(("fsdp", "ctx"), "tp"),
        P(("fsdp", "ctx"), "tp"),
        P(("fsdp", "ctx"), "tp"),
        P("tp", ("fsdp", "ctx")),
        P(("fsdp", "ctx"), "tp"),
        P(("fsdp", "ctx"), "tp"),
        P(("fsdp", "ctx"), "tp"),
        P("tp", ("fsdp", "ctx")),
        P(("fsdp", "ctx"), "tp"),
        P("tp", ("fsdp", "ctx")),
    )
    return jax.shard_map(
        body,
        mesh=mesh,
        in_specs=placed,
        out_specs=(
            P("fsdp", "ctx", None),
            P("fsdp", "ctx", None),
            P("fsdp", "ctx", None),
            P(None, ("fsdp", "ctx")),
            P(None, ("fsdp", "ctx")),
            P(("fsdp", "ctx"), "tp"),
            P(("fsdp", "ctx"), "tp"),
            P(("fsdp", "ctx"), "tp"),
            P("tp", ("fsdp", "ctx")),
            P(("fsdp", "ctx"), "tp"),
            P(("fsdp", "ctx"), "tp"),
            P(("fsdp", "ctx"), "tp"),
            P("tp", ("fsdp", "ctx")),
            P(("fsdp", "ctx"), "tp"),
            P("tp", ("fsdp", "ctx")),
        ),
        check_vma=False,
    )
```

profile of v0, /device:TPU:0, one launch (start us, length us, event | category | flops | bytes accessed | tf_op | source)
XLA Modules:
  0.0 2395.3 jit_solution(11625326553654463071)
XLA Ops:
  9.5 42.7 %all-gather = bf16[16,64,4]{1,2,0:T(4,128)(2,1)S(1)} all-gather(bf16[1,64,4]{1,2,0:T(4,128)(2,1)} %bitcast.370), channel_id=1, replica_groups=mesh['fsdp'=4,'ctx'=4,'tp'=2] {'fsdp','ctx'}, dimensions={0}, use_global_device_ids=true | all-gather | bytes 8704 | tf_op jit(solution)/shard_map/all_gather | solution.py:22
  52.3 35.8 %all-gather.1 = bf16[16,64,4]{1,2,0:T(4,128)(2,1)S(1)} all-gather(bf16[1,64,4]{1,2,0:T(4,128)(2,1)} %bitcast.371), channel_id=1, replica_groups=mesh['fsdp'=4,'ctx'=4,'tp'=2] {'fsdp','ctx'}, dimensions={0}, use_global_device_ids=true | all-gather | bytes 8704 | tf_op jit(solution)/shard_map/all_gather | solution.py:23
  94.2 31.8 %all-gather.15.cloned.1.call-done = bf16[1024,512]{1,0:T(8,128)(2,1)} async-done(((bf16[64,512]{1,0:T(8,128)(2,1)}), bf16[1024,512]{1,0:T(8,128)(2,1)}) %all-gather.15.cloned.1.call-update) | async-done | bytes 1048592 | tf_op jit(solution)/shard_map/all_gather | solution.py:26
  130.9 52.0 %all-gather.23.cloned.1.call-done = bf16[1024,512]{1,0:T(8,128)(2,1)} async-done(((bf16[64,512]{1,0:T(8,128)(2,1)}), bf16[1024,512]{1,0:T(8,128)(2,1)}) %all-gather.23.cloned.1.call-update) | async-done | bytes 1048592 | tf_op jit(solution)/shard_map/all_gather | solution.py:24
  185.1 44.6 %all-gather.21.cloned.1.call-done = bf16[2048,512]{1,0:T(8,128)(2,1)} async-done(((bf16[512,512]{1,0:T(8,128)(2,1)}), bf16[2048,512]{1,0:T(8,128)(2,1)}) %all-gather.21.cloned.1.call-update) | async-done | bytes 2097168 | tf_op jit(solution)/shard_map/all_gather | solution.py:320
  232.6 41.3 %while.111 = (s32[]{:T(128)}, f32[8,512]{1,0:T(8,128)S(1)}, f32[8,512]{1,0:T(8,128)S(1)}, s32[]{:T(128)}, bf16[2048,8,64]{0,2,1:T(8,128)(2,1)S(1)}, /*index=5*/b...) while((s32[]{:T(128)}, f32[8,512]{1,0:T(8,128)S(1)}, ...), condition=%wide.region_5.6_spmd.clone, body=%wide.region_2.5_spmd.clone.sunk | while | flops 285759488 | bytes 18834616 | solution.py:127
  280.2 22.7 while.112
  304.9 28.2 %all-gather.25.cloned.1.call-done = bf16[512,1024]{0,1:T(8,128)(2,1)} async-done(((bf16[512,64]{0,1:T(8,128)(2,1)}), bf16[512,1024]{0,1:T(8,128)(2,1)}) %all-gather.25.cloned.1.call-update) | async-done | bytes 1048592 | tf_op jit(solution)/shard_map/all_gather | solution.py:27
  338.4 51.6 %all-gather.31.cloned.1.call-done = bf16[1024,512]{1,0:T(8,128)(2,1)} async-done(((bf16[64,512]{1,0:T(8,128)(2,1)}), bf16[1024,512]{1,0:T(8,128)(2,1)}) %all-gather.31.cloned.1.call-update) | async-done | bytes 1048592 | tf_op jit(solution)/shard_map/all_gather | solution.py:29
  406.0 40.9 %all-gather.27.cloned.1.call-done = bf16[1024,512]{1,0:T(8,128)(2,1)} async-done(((bf16[64,512]{1,0:T(8,128)(2,1)}), bf16[1024,512]{1,0:T(8,128)(2,1)}) %all-gather.27.cloned.1.call-update) | async-done | bytes 1048592 | tf_op jit(solution)/shard_map/all_gather | solution.py:30
  473.7 55.7 %all-gather.29.cloned.1.call-done = bf16[1024,512]{1,0:T(8,128)(2,1)} async-done(((bf16[64,512]{1,0:T(8,128)(2,1)}), bf16[1024,512]{1,0:T(8,128)(2,1)}) %all-gather.29.cloned.1.call-update) | async-done | bytes 1048592 | tf_op jit(solution)/shard_map/all_gather | solution.py:28
  537.9 48.9 %all-gather.33.cloned.1.call-done = bf16[512,1024]{0,1:T(8,128)(2,1)} async-done(((bf16[512,64]{0,1:T(8,128)(2,1)}), bf16[512,1024]{0,1:T(8,128)(2,1)}) %all-gather.33.cloned.1.call-update) | async-done | bytes 1048592 | tf_op jit(solution)/shard_map/all_gather | solution.py:31
  614.5 75.7 %all-gather.35.cloned.1.call-done = bf16[1024,2048]{1,0:T(8,128)(2,1)} async-done(((bf16[64,2048]{1,0:T(8,128)(2,1)}), bf16[1024,2048]{1,0:T(8,128)(2,1)}) %all-gather.35.cloned.1.call-update) | async-done | bytes 4194320 | tf_op jit(solution)/shard_map/all_gather | solution.py:32
  697.5 69.7 %all-gather.37.cloned.1.call-done = bf16[2048,1024]{0,1:T(8,128)(2,1)} async-done(((bf16[2048,64]{0,1:T(8,128)(2,1)}), bf16[2048,1024]{0,1:T(8,128)(2,1)}) %all-gather.37.cloned.1.call-update) | async-done | bytes 4194320 | tf_op jit(solution)/shard_map/all_gather | solution.py:33
  812.9 22.5 all-reduce.14.cloned.1.call-done
  883.2 29.8 %while.113 = (s32[]{:T(128)}, f32[8,512]{1,0:T(8,128)S(1)}, s32[]{:T(128)}, bf16[2048,8,64]{0,2,1:T(8,128)(2,1)S(1)}, bf16[512,8,64]{0,2,1:T(8,128)(2,1)S(1)}, /...) while((s32[]{:T(128)}, f32[8,512]{1,0:T(8,128)S(1)}, ...), condition=%wide.region_30.31_spmd.clone, body=%wide.region_28.30_spmd.clone.sunk | while | flops 547887104 | bytes 19555560 | solution.py:127
  918.0 92.5 %while.136 = (s32[]{:T(128)}, f32[512,8,64]{0,2,1:T(8,128)}, f32[2048,8,64]{0,2,1:T(8,128)}, f32[2048,8,64]{0,2,1:T(8,128)}, bf16[2048,8,64]{0,2,1:T(8,128)(2,1)...) while((s32[]{:T(128)}, f32[512,8,64]{0,2,1:T(8,128)}, ...), condition=%wide.region_32.33_spmd.clone, body=%wide.region_31.32_spmd.clone.sunk | while | flops 1365248000 | bytes 99018088 | solution.py:127
  1017.3 71.2 %reduce-scatter.29.cloned.1.call-done = f32[512,512]{0,1:T(8,128)} async-done(((f32[2048,512]{0,1:T(8,128)}), f32[512,512]{0,1:T(8,128)}) %reduce-scatter.29.cloned.1.call-update) | async-done | bytes 1048592 | tf_op jit(solution)/shard_map/reduce_scatter | solution.py:66
  1092.1 76.0 %reduce-scatter.31.cloned.1.call-done = f32[512,512]{0,1:T(8,128)} async-done(((f32[2048,512]{0,1:T(8,128)}), f32[512,512]{0,1:T(8,128)}) %reduce-scatter.31.cloned.1.call-update) | async-done | bytes 1048592 | tf_op jit(solution)/shard_map/reduce_scatter | solution.py:67
  1172.6 22.2 all-reduce.18.cloned.1.call-done
  1252.3 25.5 %reduce-scatter.55.cloned.1.call-done = f32[64,4]{1,0:T(8,128)} async-done(((f32[1024,4]{1,0:T(8,128)}), f32[64,4]{1,0:T(8,128)}) %reduce-scatter.55.cloned.1.call-update) | async-done | bytes 1040
  1279.2 74.1 %reduce-scatter.53.cloned.1.call-done = f32[64,4]{1,0:T(8,128)} async-done(((f32[1024,4]{1,0:T(8,128)}), f32[64,4]{1,0:T(8,128)}) %reduce-scatter.53.cloned.1.call-update) | async-done | bytes 1040
  1354.7 82.3 %reduce-scatter.41.cloned.1.call-done = f32[64,512]{1,0:T(8,128)} async-done(((f32[1024,512]{1,0:T(8,128)}), f32[64,512]{1,0:T(8,128)}) %reduce-scatter.41.cloned.1.call-update) | async-done | bytes 131088 | tf_op jit(solution)/shard_map/reduce_scatter | solution.py:46
  1437.0 83.5 %reduce-scatter.43.cloned.1.call-done = f32[512,64]{0,1:T(8,128)} async-done(((f32[512,1024]{0,1:T(8,128)}), f32[512,64]{0,1:T(8,128)}) %reduce-scatter.43.cloned.1.call-update) | async-done | bytes 131088 | tf_op jit(solution)/shard_map/reduce_scatter | solution.py:49
  1520.5 83.9 %reduce-scatter.59.cloned.1.call-done = f32[64,512]{1,0:T(8,128)} async-done(((f32[1024,512]{1,0:T(8,128)}), f32[64,512]{1,0:T(8,128)}) %reduce-scatter.59.cloned.1.call-update) | async-done | bytes 131088
  1604.4 83.7 %reduce-scatter.57.cloned.1.call-done = f32[64,512]{1,0:T(8,128)} async-done(((f32[1024,512]{1,0:T(8,128)}), f32[64,512]{1,0:T(8,128)}) %reduce-scatter.57.cloned.1.call-update) | async-done | bytes 131088
  1688.1 83.8 %reduce-scatter.33.cloned.1.call-done = f32[64,512]{1,0:T(8,128)} async-done(((f32[1024,512]{1,0:T(8,128)}), f32[64,512]{1,0:T(8,128)}) %reduce-scatter.33.cloned.1.call-update) | async-done | bytes 131088 | tf_op jit(solution)/shard_map/reduce_scatter | solution.py:42
  1771.9 83.6 %reduce-scatter.39.cloned.1.call-done = f32[512,64]{0,1:T(8,128)} async-done(((f32[512,1024]{0,1:T(8,128)}), f32[512,64]{0,1:T(8,128)}) %reduce-scatter.39.cloned.1.call-update) | async-done | bytes 131088 | tf_op jit(solution)/shard_map/reduce_scatter | solution.py:45
  1855.5 83.7 %reduce-scatter.35.cloned.1.call-done = f32[64,512]{1,0:T(8,128)} async-done(((f32[1024,512]{1,0:T(8,128)}), f32[64,512]{1,0:T(8,128)}) %reduce-scatter.35.cloned.1.call-update) | async-done | bytes 131088 | tf_op jit(solution)/shard_map/reduce_scatter | solution.py:43
  1939.2 83.6 %reduce-scatter.37.cloned.1.call-done = f32[64,512]{1,0:T(8,128)} async-done(((f32[1024,512]{1,0:T(8,128)}), f32[64,512]{1,0:T(8,128)}) %reduce-scatter.37.cloned.1.call-update) | async-done | bytes 131088 | tf_op jit(solution)/shard_map/reduce_scatter | solution.py:44
  2022.8 181.8 %reduce-scatter.47.cloned.1.call-done = f32[2048,64]{0,1:T(8,128)} async-done(((f32[2048,1024]{0,1:T(8,128)}), f32[2048,64]{0,1:T(8,128)}) %reduce-scatter.47.cloned.1.call-update) | async-done | bytes 524304 | tf_op jit(solution)/shard_map/reduce_scatter | solution.py:51
  2204.5 182.7 %reduce-scatter.45.cloned.1.call-done = f32[64,2048]{1,0:T(8,128)} async-done(((f32[1024,2048]{1,0:T(8,128)}), f32[64,2048]{1,0:T(8,128)}) %reduce-scatter.45.cloned.1.call-update) | async-done | bytes 524304 | tf_op jit(solution)/shard_map/reduce_scatter | solution.py:50
  (518 shorter events, 475.4 us)
Async XLA Ops:
  7.2 84.1 %all-gather.19.cloned.1.call-start = ((), (), s32[]{:S(2)}) async-start(), calls=%async_computation.18 | async-start | bytes 1114112 | tf_op jit(solution)/shard_map/all_gather | solution.py:25
  7.9 118.0 %all-gather.15.cloned.1.call-start = ((), (), s32[]{:S(2)}) async-start(), calls=%async_computation.16 | async-start | bytes 1114112 | tf_op jit(solution)/shard_map/all_gather | solution.py:26
  8.7 174.2 %all-gather.23.cloned.1.call-start = ((), (), s32[]{:S(2)}) async-start(), calls=%async_computation.20 | async-start | bytes 1114112 | tf_op jit(solution)/shard_map/all_gather | solution.py:24
  9.4 220.2 %all-gather.21.cloned.1.call-start = ((), (), s32[]{:S(2)}) async-start(), calls=%async_computation.19 | async-start | bytes 2621440 | tf_op jit(solution)/shard_map/all_gather | solution.py:320
  94.1 182.2 %all-gather.17.cloned.1.call-start = ((), (), s32[]{:S(2)}) async-start(), calls=%async_computation.17 | async-start | bytes 2621440 | tf_op jit(solution)/shard_map/all_gather | solution.py:321
  128.7 204.3 %all-gather.25.cloned.1.call-start = ((), (), s32[]{:S(2)}) async-start(), calls=%async_computation.21 | async-start | bytes 1114112 | tf_op jit(solution)/shard_map/all_gather | solution.py:27
  129.3 260.7 %all-gather.31.cloned.1.call-start = ((), (), s32[]{:S(2)}) async-start(), calls=%async_computation.25 | async-start | bytes 1114112 | tf_op jit(solution)/shard_map/all_gather | solution.py:29
  130.1 316.9 %all-gather.27.cloned.1.call-start = ((), (), s32[]{:S(2)}) async-start(), calls=%async_computation.23 | async-start | bytes 1114112 | tf_op jit(solution)/shard_map/all_gather | solution.py:30
  130.8 339.1 %all-reduce.8.cloned.1.call-start = ((), (), s32[]{:S(2)}) async-start(), calls=%async_computation.22 | async-start | bytes 4194304 | tf_op jit(solution)/shard_map/psum | solution.py:57
  336.4 193.1 %all-gather.29.cloned.1.call-start = ((), (), s32[]{:S(2)}) async-start(), calls=%async_computation.24 | async-start | bytes 1114112 | tf_op jit(solution)/shard_map/all_gather | solution.py:28
  337.0 249.8 %all-gather.33.cloned.1.call-start = ((), (), s32[]{:S(2)}) async-start(), calls=%async_computation.26 | async-start | bytes 1114112 | tf_op jit(solution)/shard_map/all_gather | solution.py:31
  337.7 272.6 %all-reduce.10.cloned.1.call-start = ((), (), s32[]{:S(2)}) async-start(), calls=%async_computation.27 | async-start | bytes 4194304 | tf_op jit(solution)/shard_map/psum | solution.py:57
  590.2 100.0 %all-gather.35.cloned.1.call-start = ((), (), s32[]{:S(2)}) async-start(), calls=%async_computation.28 | async-start | bytes 4456448 | tf_op jit(solution)/shard_map/all_gather | solution.py:32
  590.9 176.3 %all-gather.37.cloned.1.call-start = ((), (), s32[]{:S(2)}) async-start(), calls=%async_computation.29 | async-start | bytes 4456448 | tf_op jit(solution)/shard_map/all_gather | solution.py:33
  591.5 203.1 %all-reduce.12.cloned.1.call-start = ((), (), s32[]{:S(2)}) async-start(), calls=%async_computation.30 | async-start | bytes 4194304 | tf_op jit(solution)/shard_map/psum | solution.py:57
  852.4 159.1 %reduce-scatter.51.cloned.1.call-start = ((), (), s32[]{:S(2)}) async-start(), calls=%async_computation.44 | async-start | bytes 655360
  857.8 154.8 %reduce-scatter.49.cloned.1.call-start = ((), (), s32[]{:S(2)}) async-start(), calls=%async_computation.43 | async-start | bytes 655360
  861.5 227.0 %reduce-scatter.29.cloned.1.call-start = ((), (), s32[]{:S(2)}) async-start(), calls=%async_computation.33 | async-start | bytes 5242880 | tf_op jit(solution)/shard_map/reduce_scatter | solution.py:66
  1010.4 157.7 %reduce-scatter.31.cloned.1.call-start = ((), (), s32[]{:S(2)}) async-start(), calls=%async_computation.34 | async-start | bytes 5242880 | tf_op jit(solution)/shard_map/reduce_scatter | solution.py:67
  1011.2 183.6 %all-reduce.18.cloned.1.call-start = ((), (), s32[]{:S(2)}) async-start(), calls=%async_computation.49 | async-start | bytes 4718592 | tf_op jit(solution)/shard_map/psum | solution.py:61
  1172.5 105.3 %reduce-scatter.55.cloned.1.call-start = ((), (), s32[]{:S(2)}) async-start(), calls=%async_computation.46 | async-start | bytes 557056
  1199.5 153.8 %reduce-scatter.53.cloned.1.call-start = ((), (), s32[]{:S(2)}) async-start(), calls=%async_computation.45 | async-start | bytes 557056
  1200.7 236.4 %reduce-scatter.41.cloned.1.call-start = ((), (), s32[]{:S(2)}) async-start(), calls=%async_computation.39 | async-start | bytes 2228224 | tf_op jit(solution)/shard_map/reduce_scatter | solution.py:46
  1204.2 316.4 %reduce-scatter.43.cloned.1.call-start = ((), (), s32[]{:S(2)}) async-start(), calls=%async_computation.40 | async-start | bytes 2228224 | tf_op jit(solution)/shard_map/reduce_scatter | solution.py:49
  1207.9 396.5 %reduce-scatter.59.cloned.1.call-start = ((), (), s32[]{:S(2)}) async-start(), calls=%async_computation.48 | async-start | bytes 2228224
  1210.2 477.9 %reduce-scatter.57.cloned.1.call-start = ((), (), s32[]{:S(2)}) async-start(), calls=%async_computation.47 | async-start | bytes 2228224
  1212.6 559.3 %reduce-scatter.33.cloned.1.call-start = ((), (), s32[]{:S(2)}) async-start(), calls=%async_computation.35 | async-start | bytes 2228224 | tf_op jit(solution)/shard_map/reduce_scatter | solution.py:42
  1216.1 639.3 %reduce-scatter.39.cloned.1.call-start = ((), (), s32[]{:S(2)}) async-start(), calls=%async_computation.38 | async-start | bytes 2228224 | tf_op jit(solution)/shard_map/reduce_scatter | solution.py:45
  1219.8 719.4 %reduce-scatter.35.cloned.1.call-start = ((), (), s32[]{:S(2)}) async-start(), calls=%async_computation.36 | async-start | bytes 2228224 | tf_op jit(solution)/shard_map/reduce_scatter | solution.py:43
  1223.7 799.1 %reduce-scatter.37.cloned.1.call-start = ((), (), s32[]{:S(2)}) async-start(), calls=%async_computation.37 | async-start | bytes 2228224 | tf_op jit(solution)/shard_map/reduce_scatter | solution.py:44
  1227.2 977.3 %reduce-scatter.47.cloned.1.call-start = ((), (), s32[]{:S(2)}) async-start(), calls=%async_computation.42 | async-start | bytes 8912896 | tf_op jit(solution)/shard_map/reduce_scatter | solution.py:51
  1237.7 1149.6 %reduce-scatter.45.cloned.1.call-start = ((), (), s32[]{:S(2)}) async-start(), calls=%async_computation.41 | async-start | bytes 8912896 | tf_op jit(solution)/shard_map/reduce_scatter | solution.py:50
  (117 other events, 4647.7 us)
Sparse Core Ops, SparseCore 0:
  10.8 58.1 all-gather.18
  71.7 54.1 all-gather.14
  128.7 54.1 all-gather.22
  184.9 44.7 all-gather.20
  231.6 44.6 all-gather.16
  278.9 54.0 all-gather.24
  335.8 54.1 all-gather.30
  392.7 54.1 all-gather.26
  449.9 20.0 all-reduce.7
  472.9 56.5 all-gather.28
  532.6 54.1 all-gather.32
  590.3 20.0 all-reduce.9
  613.1 77.0 all-gather.34
  692.8 74.3 all-gather.36
  813.0 22.3 all-reduce.13
  852.5 22.3 all-reduce.15
  877.2 22.8 reduce-scatter.50
  1010.6 77.9 reduce-scatter.28
  1090.8 77.2 reduce-scatter.30
  1172.6 22.1 all-reduce.17
  1199.6 78.1 reduce-scatter.54
  1280.0 73.2 reduce-scatter.52
  1356.2 80.7 reduce-scatter.40
  1439.7 80.7 reduce-scatter.42
  1523.2 81.1 reduce-scatter.58
  1607.2 80.8 reduce-scatter.56
  1690.9 80.8 reduce-scatter.32
  1774.6 80.8 reduce-scatter.38
  1858.3 80.8 reduce-scatter.34
  1942.1 80.6 reduce-scatter.36
  2025.5 178.9 reduce-scatter.46
  2207.4 179.8 reduce-scatter.44
  (2 shorter events, 39.5 us)
where the time goes:
time: 2410 us; the launch traced here: 2400 us
  waiting for transfers between devices  1890 us (78%)
  matrix products  243 us (10%)
  blocking collectives  107 us (4%)
  other arithmetic  73.9 us (3%)
  local copies, waits for them, and re-layouts  60.1 us (2%)
    unnamed x40, waiting for transfers between devices  275 us
    reduce_scatter x1, waiting for transfers between devices, return_grads(): lax.psum_scatter(grads[10], ('fsdp', 'ctx'), scatter_dimension=0, tiled=T...  183 us
    reduce_scatter x1, waiting for transfers between devices, return_grads(): lax.psum_scatter(grads[11], ('fsdp', 'ctx'), scatter_dimension=1, tiled=T...  182 us
    reduce_scatter x1, waiting for transfers between devices, return_grads(): lax.psum_scatter(grads[2], ('fsdp', 'ctx'), scatter_dimension=0, tiled=True)  83.8 us
    reduce_scatter x1, waiting for transfers between devices, return_grads(): lax.psum_scatter(grads[3], ('fsdp', 'ctx'), scatter_dimension=0, tiled=True)  83.7 us
    reduce_scatter x1, waiting for transfers between devices, return_grads(): lax.psum_scatter(grads[5], ('fsdp', 'ctx'), scatter_dimension=1, tiled=True)  83.6 us
    reduce_scatter x1, waiting for transfers between devices, return_grads(): lax.psum_scatter(grads[4], ('fsdp', 'ctx'), scatter_dimension=0, tiled=True)  83.6 us
    reduce_scatter x1, waiting for transfers between devices, return_grads(): lax.psum_scatter(grads[9], ('fsdp', 'ctx'), scatter_dimension=1, tiled=True)  83.5 us
  transfers between devices with their start and end apart: 34, of which 31 were waited for; matrix products, arithmetic and copies ran while one was open for 12% of the time, Pallas kernels for 0%

commit v1 on v0

v1 whole, which is shorter than its diff:
```python
import functools

import jax
import jax.numpy as jnp
from jax import lax
from jax.experimental import pallas as pl
from jax.experimental.pallas import tpu as pltpu
from jax.sharding import PartitionSpec as P

HEAD_DIM = 64
PAIR = 2 * HEAD_DIM
EPS = 1e-05
GELU_A = 0.7978845608028654
GELU_B = 0.044715
BF = jnp.bfloat16
F32 = jnp.float32
LOW = -1e30


def nn(left, right):
    return jnp.dot(left, right, preferred_element_type=F32)


def tn(left, right):
    return lax.dot_general(left, right, (((0,), (0,)), ((), ())), preferred_element_type=F32)


def nt(left, right):
    return lax.dot_general(left, right, (((1,), (1,)), ((), ())), preferred_element_type=F32)


def smooth_gate(values):
    return 0.5 * values * (1.0 + jnp.tanh(GELU_A * (values + GELU_B * values * values * values)))


def norm_parts(values):
    mean = jnp.mean(values, axis=-1, keepdims=True)
    centred = values - mean
    scale = lax.rsqrt(jnp.mean(centred * centred, axis=-1, keepdims=True) + EPS)
    return (centred * scale, scale)


def norm_back(grad_result, normed, scale, gain):
    grad_normed = grad_result * gain
    grad_input = scale * (
        grad_normed
        - jnp.mean(grad_normed, axis=-1, keepdims=True)
        - normed * jnp.mean(grad_normed * normed, axis=-1, keepdims=True)
    )
    return (grad_input, jnp.sum(grad_result * normed, axis=0), jnp.sum(grad_result, axis=0))


def shift(value, axis, step):
    n = lax.axis_size(axis)
    return lax.ppermute(value, axis, [(i, (i + step) % n) for i in range(n)])


def swap(value):
    return shift(value, "tp", 1)


def in_order(pieces, axis):
    n = len(pieces)
    me = lax.axis_index(axis)
    return [lax.select_n(me, *[pieces[(m - j) % n] for m in range(n)]) for j in range(n)]


def gather_direct(value, axis):
    n = lax.axis_size(axis)
    return [value] + [shift(value, axis, s) for s in range(1, n)]


def gather_line(value, axis):
    n = lax.axis_size(axis)
    me = lax.axis_index(axis)
    ups, downs = [value], [value]
    for s in range(1, n):
        ups.append(lax.ppermute(ups[-1], axis, [(i, i + 1) for i in range(s - 1, n - 1)]))
        downs.append(lax.ppermute(downs[-1], axis, [(i, i - 1) for i in range(1, n - s + 1)]))
    return [value] + [jnp.where(me >= s, ups[s], downs[n - s]) for s in range(1, n)]


def exchange_direct(blocks, axis):
    n = lax.axis_size(axis)
    me = lax.axis_index(axis)

    def pick(d):
        return lax.dynamic_index_in_dim(blocks, d, 0, keepdims=False)

    return [pick(me)] + [shift(pick((me + s) % n), axis, s) for s in range(1, n)]


def total(pieces):
    out = pieces[0].astype(F32)
    for piece in pieces[1:]:
        out = out + piece.astype(F32)
    return out


def bits_of(axis, low_first):
    n = lax.axis_size(axis)
    order = list(range(n.bit_length() - 1))
    return order if low_first else order[::-1]


def gather_double(value, axis, low_first):
    n = lax.axis_size(axis)
    count = n.bit_length() - 1
    me = lax.axis_index(axis)
    held = value.reshape((1,) * count + value.shape)
    for bit in bits_of(axis, low_first):
        other = lax.ppermute(held, axis, [(i, i ^ (1 << bit)) for i in range(n)])
        mine = (me >> bit) & 1
        held = jnp.concatenate(
            [jnp.where(mine == 0, held, other), jnp.where(mine == 0, other, held)],
            axis=count - 1 - bit,
        )
    return held.reshape((n * value.shape[0],) + value.shape[1:])


def scatter_double(value, axis, low_first):
    n = lax.axis_size(axis)
    count = n.bit_length() - 1
    me = lax.axis_index(axis)
    rows = value.shape[0] // n
    held = value.reshape((2,) * count + (rows,) + value.shape[1:])
    for bit in bits_of(axis, low_first):
        dim = count - 1 - bit
        mine = (me >> bit) & 1
        away = lax.dynamic_slice_in_dim(held, 1 - mine, 1, dim)
        keep = lax.dynamic_slice_in_dim(held, mine, 1, dim)
        came = lax.ppermute(away, axis, [(i, i ^ (1 << bit)) for i in range(n)])
        held = (keep.astype(F32) + came.astype(F32)).astype(value.dtype)
    return held.reshape((rows,) + value.shape[1:])


def scatter_direct(value, axis):
    n = lax.axis_size(axis)
    blocks = value.reshape((n, value.shape[0] // n) + value.shape[1:])
    return total(exchange_direct(blocks, axis))


def fetch_rows(shard, low_first):
    held = jnp.concatenate(in_order(gather_line(shard, "ctx"), "ctx"), axis=0)
    return gather_double(held, "fsdp", low_first)


def return_rows(grad, low_first):
    return scatter_direct(scatter_double(grad, "fsdp", low_first), "ctx")


def lanes_of(head, shape):
    lane = lax.broadcasted_iota(jnp.int32, shape, len(shape) - 1)
    return (lane // HEAD_DIM) == head


def spans(count, block):
    half = block // 2
    return half


def self_forward_kernel(n, block, info, qkv, mixed, logs, q_s, k_s, v_s):
    limit, me_c, me_t = info[0], info[1], info[2]
    half = block // 2
    for c in range(n):
        for t in range(2):
            place = lax.rem(me_c - c + n, n) * block + (me_t ^ t) * half
            place = pl.multiple_of(place, half)
            to = slice(c * block + t * half, c * block + t * half + half)
            rows = qkv[pl.ds(place, half), :]
            q_s[to, :] = rows[:, :PAIR] * jnp.asarray(HEAD_DIM**-0.5, BF)
            keys = rows[:, PAIR : 2 * PAIR]
            for h in range(2):
                k_s[h, to, :] = jnp.where(lanes_of(h, keys.shape), keys, jnp.zeros_like(keys))
            v_s[:, to] = rows[:, 2 * PAIR :].astype(F32).T.astype(BF)

    def one(i, _):
        at_q = pl.multiple_of(i * block, block)
        query = q_s[pl.ds(at_q, block), :]

        def step(masked, j, state):
            at_k = pl.multiple_of(j * block, block)
            out = []
            for h in range(2):
                top, tot, acc = state[h]
                score = nt(k_s[h, pl.ds(at_k, block), :], query)
                if masked:
                    key_at = at_k + lax.broadcasted_iota(jnp.int32, score.shape, 0)
                    slot_at = at_q + lax.broadcasted_iota(jnp.int32, score.shape, 1)
                    score = jnp.where((key_at <= slot_at) & (key_at < limit), score, LOW)
                new_top = jnp.maximum(top, jnp.max(score, axis=0, keepdims=True))
                fade = jnp.exp(top - new_top)
                chance = jnp.exp(score - new_top)
                tot = tot * fade + jnp.sum(chance, axis=0, keepdims=True)
                part = nn(
                    v_s[h * HEAD_DIM : (h + 1) * HEAD_DIM, pl.ds(at_k, block)], chance.astype(BF)
                )
                out.append((new_top, tot, acc * fade + part))
            return tuple(out)

        start = tuple(
            (
                jnp.full((1, block), LOW, F32),
                jnp.zeros((1, block), F32),
                jnp.zeros((HEAD_DIM, block), F32),
            )
            for _ in range(2)
        )
        whole = jnp.minimum(i, limit // block)
        last = jnp.minimum(i + 1, (limit + block - 1) // block)
        state = lax.fori_loop(0, whole, functools.partial(step, False), start)
        state = lax.fori_loop(whole, last, functools.partial(step, True), state)
        both = jnp.concatenate([acc / tot for _, tot, acc in state], axis=0)
        place = pl.multiple_of(lax.rem(me_c - i + n, n) * block, block)
        mixed[pl.ds(place, block), :] = both.T.astype(BF)
        for h in range(2):
            top, tot, _ = state[h]
            logs[h : h + 1, pl.ds(at_q, block)] = top + jnp.log(tot)
        return 0

    lax.fori_loop(0, n, one, 0)


def self_backward_kernel(
    n, block, info, qkv, mixed, grad, logs, grads, q_s, k_s, v_s, kt_s, d_s, delta_s, dq_s
):
    limit, me_c, me_t = info[0], info[1], info[2]
    half = block // 2
    for c in range(n):
        for t in range(2):
            place = lax.rem(me_c - c + n, n) * block + (me_t ^ t) * half
            place = pl.multiple_of(place, half)
            to = slice(c * block + t * half, c * block + t * half + half)
            rows = qkv[pl.ds(place, half), :]
            q_s[to, :] = rows[:, :PAIR] * jnp.asarray(HEAD_DIM**-0.5, BF)
            keys = rows[:, PAIR : 2 * PAIR]
            values = rows[:, 2 * PAIR :]
            for h in range(2):
                k_s[h, to, :] = jnp.where(lanes_of(h, keys.shape), keys, jnp.zeros_like(keys))
                v_s[h, to, :] = jnp.where(lanes_of(h, keys.shape), values, jnp.zeros_like(keys))
            kt_s[:, to] = keys.astype(F32).T.astype(BF)
            at = pl.multiple_of(lax.rem(me_c - c + n, n) * block + t * half, half)
            dout = grad[pl.ds(at, half), :]
            d_s[to, :] = dout
            both = (dout.astype(F32) * mixed[pl.ds(at, half), :].astype(F32)).T
            for h in range(2):
                delta_s[h : h + 1, to] = jnp.sum(
                    both[h * HEAD_DIM : (h + 1) * HEAD_DIM, :], axis=0, keepdims=True
                )
    dq_s[...] = jnp.zeros_like(dq_s)

    def one(j, _):
        at_k = pl.multiple_of(j * block, block)

        def step(masked, i, state):
            at_q = pl.multiple_of(i * block, block)
            query = q_s[pl.ds(at_q, block), :]
            dout = d_s[pl.ds(at_q, block), :]
            out = []
            for h in range(2):
                dk, dv = state[h]
                score = nt(k_s[h, pl.ds(at_k, block), :], query)
                if masked:
                    key_at = at_k + lax.broadcasted_iota(jnp.int32, score.shape, 0)
                    slot_at = at_q + lax.broadcasted_iota(jnp.int32, score.shape, 1)
                    score = jnp.where((key_at <= slot_at) & (key_at < limit), score, LOW)
                chance = jnp.exp(score - logs[h : h + 1, pl.ds(at_q, block)])
                slopes = nt(v_s[h, pl.ds(at_k, block), :], dout)
                bend = (chance * (slopes - delta_s[h : h + 1, pl.ds(at_q, block)])).astype(BF)
                dv = dv + nn(chance.astype(BF), dout)
                dk = dk + nn(bend, query)
                side = slice(h * HEAD_DIM, (h + 1) * HEAD_DIM)
                dq_s[side, pl.ds(at_q, block)] += nn(kt_s[side, pl.ds(at_k, block)], bend)
                out.append((dk, dv))
            return tuple(out)

        start = tuple(
            (jnp.zeros((block, PAIR), F32), jnp.zeros((block, PAIR), F32)) for _ in range(2)
        )
        end = jnp.where(j * block < limit, n, j)
        middle = jnp.where((j + 1) * block <= limit, jnp.minimum(j + 1, end), end)
        state = lax.fori_loop(j, middle, functools.partial(step, True), start)
        state = lax.fori_loop(middle, end, functools.partial(step, False), state)
        first_head = lanes_of(0, (block, PAIR))
        dk = jnp.where(first_head, state[0][0], state[1][0]).astype(BF)
        dv = jnp.where(first_head, state[0][1], state[1][1]).astype(BF)
        for t in range(2):
            place = lax.rem(me_c - j + n, n) * block + (me_t ^ t) * half
            place = pl.multiple_of(place, half)
            grads[pl.ds(place, half), PAIR : 2 * PAIR] = dk[t * half : (t + 1) * half, :]
            grads[pl.ds(place, half), 2 * PAIR :] = dv[t * half : (t + 1) * half, :]
        return 0

    lax.fori_loop(0, n, one, 0)
    for c in range(n):
        dq = (dq_s[:, c * block : (c + 1) * block] * HEAD_DIM**-0.5).T.astype(BF)
        for t in range(2):
            place = lax.rem(me_c - c + n, n) * block + (me_t ^ t) * half
            place = pl.multiple_of(place, half)
            grads[pl.ds(place, half), :PAIR] = dq[t * half : (t + 1) * half, :]


def cross_scores(limit, keys, query):
    score = nt(keys, query)
    key_at = lax.broadcasted_iota(jnp.int32, score.shape, 0)
    return jnp.where(key_at < limit, score, LOW)


def masked_pair(values, head):
    return jnp.where(lanes_of(head, values.shape), values, jnp.zeros_like(values))


def cross_forward_kernel(info, query_ref, kv, mixed, logs):
    limit = info[0]
    query = query_ref[...] * jnp.asarray(HEAD_DIM**-0.5, BF)
    keys = kv[0, :, :PAIR]
    values = kv[0, :, PAIR:].astype(F32).T.astype(BF)
    outs = []
    for h in range(2):
        score = cross_scores(limit, masked_pair(keys, h), query)
        top = jnp.max(score, axis=0, keepdims=True)
        chance = jnp.exp(score - top)
        tot = jnp.sum(chance, axis=0, keepdims=True)
        outs.append(nn(values[h * HEAD_DIM : (h + 1) * HEAD_DIM, :], chance.astype(BF)) / tot)
        logs[0, h : h + 1, :] = top + jnp.log(tot)
    mixed[...] = jnp.concatenate(outs, axis=0).T.astype(BF)


def cross_backward_kernel(info, query_ref, kv, mixed, grad, logs, dq_ref, dkv):
    limit = info[0]
    query = query_ref[...] * jnp.asarray(HEAD_DIM**-0.5, BF)
    keys = kv[0, :, :PAIR]
    values = kv[0, :, PAIR:]
    keys_t = keys.astype(F32).T.astype(BF)
    dout = grad[...]
    both = (dout.astype(F32) * mixed[...].astype(F32)).T
    dqs, dks, dvs = [], [], []
    for h in range(2):
        side = slice(h * HEAD_DIM, (h + 1) * HEAD_DIM)
        delta = jnp.sum(both[side, :], axis=0, keepdims=True)
        score = cross_scores(limit, masked_pair(keys, h), query)
        chance = jnp.exp(score - logs[0, h : h + 1, :])
        slopes = nt(masked_pair(values, h), dout)
        bend = (chance * (slopes - delta)).astype(BF)
        dvs.append(nn(chance.astype(BF), dout))
        dks.append(nn(bend, query))
        dqs.append(nn(keys_t[side, :], bend))
    dq_ref[...] = (jnp.concatenate(dqs, axis=0) * HEAD_DIM**-0.5).T.astype(BF)
    first_head = lanes_of(0, dks[0].shape)
    dkv[0, :, :PAIR] = jnp.where(first_head, dks[0], dks[1]).astype(BF)
    dkv[0, :, PAIR:] = jnp.where(first_head, dvs[0], dvs[1]).astype(BF)


VMEM_LIMIT = 48 * 1024 * 1024


def vmem_spec():
    return pl.BlockSpec(memory_space=pltpu.VMEM)


def smem_spec():
    return pl.BlockSpec(memory_space=pltpu.SMEM)


def self_forward(info, qkv, n):
    slots = qkv.shape[0]
    block = slots // n
    pairs = slots * slots
    return pl.pallas_call(
        functools.partial(self_forward_kernel, n, block),
        out_shape=(
            jax.ShapeDtypeStruct((slots, PAIR), BF),
            jax.ShapeDtypeStruct((2, slots), F32),
        ),
        in_specs=[smem_spec(), vmem_spec()],
        out_specs=(vmem_spec(), vmem_spec()),
        scratch_shapes=[
            pltpu.VMEM((slots, PAIR), BF),
            pltpu.VMEM((2, slots, PAIR), BF),
            pltpu.VMEM((PAIR, slots), BF),
        ],
        compiler_params=pltpu.CompilerParams(vmem_limit_bytes=VMEM_LIMIT),
        cost_estimate=pl.CostEstimate(
            flops=pairs * PAIR * 4, transcendentals=pairs, bytes_accessed=slots * PAIR * 8
        ),
        name="self_forward",
    )(info, qkv)


def self_backward(info, qkv, mixed, grad, logs, n):
    slots = qkv.shape[0]
    block = slots // n
    pairs = slots * slots
    return pl.pallas_call(
        functools.partial(self_backward_kernel, n, block),
        out_shape=jax.ShapeDtypeStruct((slots, 3 * PAIR), BF),
        in_specs=[smem_spec()] + [vmem_spec()] * 4,
        out_specs=vmem_spec(),
        scratch_shapes=[
            pltpu.VMEM((slots, PAIR), BF),
            pltpu.VMEM((2, slots, PAIR), BF),
            pltpu.VMEM((2, slots, PAIR), BF),
            pltpu.VMEM((PAIR, slots), BF),
            pltpu.VMEM((slots, PAIR), BF),
            pltpu.VMEM((2, slots), F32),
            pltpu.VMEM((PAIR, slots), F32),
        ],
        compiler_params=pltpu.CompilerParams(vmem_limit_bytes=VMEM_LIMIT),
        cost_estimate=pl.CostEstimate(
            flops=pairs * PAIR * 10, transcendentals=pairs, bytes_accessed=slots * PAIR * 20
        ),
        name="self_backward",
    )(info, qkv, mixed, grad, logs)


def cross_forward(info, query, kv, n):
    rows, keys = query.shape[0], kv.shape[1]
    pairs = rows * keys * n
    grid_spec = pltpu.PrefetchScalarGridSpec(
        num_scalar_prefetch=1,
        grid=(n,),
        in_specs=[
            pl.BlockSpec((rows, PAIR), lambda j, info: (0, j)),
            pl.BlockSpec((1, keys, 2 * PAIR), lambda j, info: (lax.rem(info[1] - j + n, n), 0, 0)),
        ],
        out_specs=[
            pl.BlockSpec((rows, PAIR), lambda j, info: (0, j)),
            pl.BlockSpec((1, 2, rows), lambda j, info: (j, 0, 0)),
        ],
    )
    return pl.pallas_call(
        cross_forward_kernel,
        grid_spec=grid_spec,
        out_shape=(
            jax.ShapeDtypeStruct((rows, PAIR * n), BF),
            jax.ShapeDtypeStruct((n, 2, rows), F32),
        ),
        compiler_params=pltpu.CompilerParams(vmem_limit_bytes=VMEM_LIMIT),
        cost_estimate=pl.CostEstimate(
            flops=pairs * PAIR * 8, transcendentals=2 * pairs, bytes_accessed=rows * PAIR * n * 6
        ),
        name="cross_forward",
    )(info, query, kv)


def cross_backward(info, query, kv, mixed, grad, logs, n):
    rows, keys = query.shape[0], kv.shape[1]
    pairs = rows * keys * n
    col = pl.BlockSpec((rows, PAIR), lambda j, info: (0, j))
    grid_spec = pltpu.PrefetchScalarGridSpec(
        num_scalar_prefetch=1,
        grid=(n,),
        in_specs=[
            col,
            pl.BlockSpec((1, keys, 2 * PAIR), lambda j, info: (lax.rem(info[1] - j + n, n), 0, 0)),
            col,
            col,
            pl.BlockSpec((1, 2, rows), lambda j, info: (j, 0, 0)),
        ],
        out_specs=[
            col,
            pl.BlockSpec((1, keys, 2 * PAIR), lambda j, info: (lax.rem(j - info[1] + n, n), 0, 0)),
        ],
    )
    return pl.pallas_call(
        cross_backward_kernel,
        grid_spec=grid_spec,
        out_shape=(
            jax.ShapeDtypeStruct((rows, PAIR * n), BF),
            jax.ShapeDtypeStruct((n, keys, 2 * PAIR), BF),
        ),
        compiler_params=pltpu.CompilerParams(vmem_limit_bytes=VMEM_LIMIT),
        cost_estimate=pl.CostEstimate(
            flops=pairs * PAIR * 20, transcendentals=2 * pairs, bytes_accessed=rows * PAIR * n * 10
        ),
        name="cross_backward",
    )(info, query, kv, mixed, grad, logs)


def tp_total(partial):
    mine = partial.astype(BF)
    return mine.astype(F32) + swap(mine).astype(F32)


def tp_join(mine):
    me = lax.axis_index("tp")
    other = swap(mine)
    return jnp.concatenate(
        [jnp.where(me == 0, mine, other), jnp.where(me == 0, other, mine)], axis=0
    )


def body(
    inputs,
    encoder_states,
    seq_lengths,
    enc_lengths,
    cotangent,
    norm_gains,
    norm_biases,
    w_query,
    w_key,
    w_value,
    w_out,
    w_cross_query,
    w_cross_key,
    w_cross_value,
    w_cross_out,
    w_inner,
    w_outer,
):
    n = lax.axis_size("ctx")
    me_c, me_t = lax.axis_index("ctx"), lax.axis_index("tp")
    rows, width = inputs.shape[1], inputs.shape[2]
    half = rows // 2
    wide = w_query.shape[1]
    shard = w_query.shape[0]
    seq_limit, enc_limit = seq_lengths[0], enc_lengths[0]
    self_info = jnp.stack([seq_limit, me_c, me_t]).astype(jnp.int32)
    cross_info = jnp.stack([enc_limit, me_c, me_t]).astype(jnp.int32)

    params = jnp.concatenate([norm_gains, norm_biases], axis=0)
    params = jnp.concatenate(in_order(gather_direct(params, "ctx"), "ctx"), axis=1)
    params = jnp.concatenate(in_order(gather_direct(params, "fsdp"), "fsdp"), axis=1)
    params = params.astype(F32)
    gains, biases = params[:4], params[4:]

    five = jnp.stack([w_query, w_key, w_value, w_cross_key, w_cross_value], axis=1)
    five = five.reshape(shard, 5, n, PAIR).transpose(2, 0, 1, 3).reshape(n, shard, 5 * PAIR)
    five = jnp.concatenate(in_order(exchange_direct(five, "ctx"), "ctx"), axis=0)
    five = jnp.concatenate(in_order(gather_direct(five, "fsdp"), "fsdp"), axis=0)
    w_qkv, w_ckv = five[:, : 3 * PAIR], five[:, 3 * PAIR :]

    hidden_x = inputs[0].astype(F32)
    normed_a, scale_a = norm_parts(hidden_x)
    attn_in = (normed_a * gains[0] + biases[0]).astype(BF)
    own = lax.dynamic_slice_in_dim(attn_in, me_t * half, half, 0)
    rest = lax.dynamic_slice_in_dim(attn_in, (1 - me_t) * half, half, 0)
    came = gather_line(own, "ctx")[1:]
    came_other = swap(jnp.concatenate(came, axis=0))
    blocks = [own, rest]
    for s in range(n - 1):
        blocks += [came[s], came_other[s * half : (s + 1) * half]]
    attn_all = jnp.concatenate(blocks, axis=0)

    enc_half = encoder_states.shape[1] // 2
    enc_own = lax.dynamic_slice_in_dim(encoder_states[0], me_t * enc_half, enc_half, 0)
    enc_came = jnp.stack(in_order(gather_direct(enc_own, "ctx"), "ctx"), axis=0)
    enc_came_other = swap(enc_came)
    enc_all = jnp.stack(
        [
            jnp.where(me_t == 0, enc_came, enc_came_other),
            jnp.where(me_t == 0, enc_came_other, enc_came),
        ],
        axis=1,
    ).reshape(-1, width)

    w_out_t = fetch_rows(w_out.T, False)
    w_cq_co = fetch_rows(jnp.concatenate([w_cross_query, w_cross_out.T], axis=1), True)
    w_cq, w_co_t = w_cq_co[:, :wide], w_cq_co[:, wide:]
    w_in = fetch_rows(w_inner, True)
    w_outer_t = fetch_rows(w_outer.T, False)

    qkv = nn(attn_all, w_qkv).astype(BF)
    mixed, logs = self_forward(self_info, qkv, n)
    pieces = [mixed[:rows]] + [
        shift(mixed[s * rows : (s + 1) * rows], "ctx", -s) for s in range(1, n)
    ]
    attn_flat = jnp.concatenate(in_order([pieces[(n - s) % n] for s in range(n)], "ctx"), axis=1)
    first = hidden_x + tp_total(nt(attn_flat, w_out_t))

    ckv_own = nn(enc_all, w_ckv).astype(BF)
    ckv = jnp.stack(gather_direct(ckv_own, "ctx"), axis=0)
    normed_c, scale_c = norm_parts(first)
    cross_in = (normed_c * gains[1] + biases[1]).astype(BF)
    cross_query = nn(cross_in, w_cq).astype(BF)
    cross_flat, cross_logs = cross_forward(cross_info, cross_query, ckv, n)
    second = first + tp_total(nt(cross_flat, w_co_t))

    normed_f, scale_f = norm_parts(second)
    ffn_in = (normed_f * gains[2] + biases[2]).astype(BF)
    inner = nn(ffn_in, w_in)
    gated, gate_pullback = jax.vjp(smooth_gate, inner)
    active = gated.astype(BF)
    third = second + tp_total(nt(active, w_outer_t))

    positions = me_c * rows + lax.iota(jnp.int32, rows)
    valid = (positions < seq_limit).astype(F32)[:, None]
    normed_y, scale_y = norm_parts(third)
    output = (normed_y * gains[3] + biases[3]) * valid

    grad_y = cotangent[0].astype(F32) * valid
    grad_third, gain_y, bias_y = norm_back(grad_y, normed_y, scale_y, gains[3])
    g3 = grad_third.astype(BF)
    grad_active = gate_pullback(nn(g3, w_outer_t))[0].astype(BF)
    grad_outer = return_rows(tn(g3, active).astype(BF), True).T
    grad_inner = return_rows(tn(ffn_in, grad_active).astype(BF), False)
    grad_ffn_in = tp_total(nt(grad_active, w_in))
    part_f, gain_f, bias_f = norm_back(grad_ffn_in, normed_f, scale_f, gains[2])
    grad_second = grad_third + part_f
    g2 = grad_second.astype(BF)

    grad_cross = nn(g2, w_co_t).astype(BF)
    grad_cq, dkv = cross_backward(
        cross_info, cross_query, ckv, cross_flat, grad_cross, cross_logs, n
    )
    grad_ckv = total([dkv[0]] + [shift(dkv[s], "ctx", s) for s in range(1, n)]).astype(BF)
    pair = jnp.concatenate(
        [tn(cross_in, grad_cq).astype(BF), tn(g2, cross_flat).astype(BF)], axis=1
    )
    pair = return_rows(pair, True)
    grad_w_cq, grad_w_co = pair[:, :wide], pair[:, wide:].T
    grad_cross_in = tp_total(nt(grad_cq, w_cq))
    part_c, gain_c, bias_c = norm_back(grad_cross_in, normed_c, scale_c, gains[1])
    grad_first = grad_second + part_c
    g1 = grad_first.astype(BF)

    enc_part = tp_total(nt(grad_ckv, w_ckv)).astype(BF).reshape(n, 2, enc_half, width)
    enc_part = lax.dynamic_index_in_dim(enc_part, me_t, 1, keepdims=False)
    grad_encoder = tp_join(total(exchange_direct(enc_part, "ctx")))

    grad_w_out = return_rows(tn(g1, attn_flat).astype(BF), False).T
    grad_attn = nn(g1, w_out_t).astype(BF)
    grad_attn = grad_attn.reshape(rows, n, PAIR).transpose(1, 0, 2)
    dmixed = jnp.concatenate(exchange_direct(grad_attn, "ctx"), axis=0)
    dqkv = self_backward(self_info, qkv, mixed, dmixed, logs, n)
    part = nt(dqkv, w_qkv).astype(BF).reshape(n, 2, half, width)
    part = (part[:, 0].astype(F32) + swap(part[:, 1]).astype(F32)).astype(BF)
    grad_attn_in = total([part[0]] + [shift(part[s], "ctx", -s) for s in range(1, n)])

    dfive = jnp.concatenate([tn(attn_all, dqkv), tn(enc_all, grad_ckv)], axis=1).astype(BF)
    f = lax.axis_size("fsdp")
    dfive = total(exchange_direct(dfive.reshape(f, n * shard, 5 * PAIR), "fsdp")).astype(BF)
    dfive = in_order(exchange_direct(dfive.reshape(n, shard, 5 * PAIR), "ctx"), "ctx")
    dfive = jnp.stack(dfive, axis=0).reshape(n, shard, 5, PAIR).transpose(2, 1, 0, 3)
    dfive = dfive.reshape(5, shard, wide).astype(F32)

    def mine(values):
        return lax.dynamic_slice_in_dim(values, me_t * half, half, 0)

    part_a, gain_a, bias_a = norm_back(grad_attn_in, mine(normed_a), mine(scale_a), gains[0])
    grad_inputs = tp_join(mine(grad_first) + part_a)
    pair_a = jnp.stack([gain_a, bias_a])
    pair_a = pair_a + swap(pair_a)
    norm_grads = jnp.stack(
        [pair_a[0], gain_c, gain_f, gain_y, pair_a[1], bias_c, bias_f, bias_y]
    )
    norm_grads = norm_grads.reshape(8, f, n * shard).transpose(1, 0, 2)
    norm_grads = total(exchange_direct(norm_grads, "fsdp"))
    norm_grads = norm_grads.reshape(8, n, shard).transpose(1, 0, 2)
    norm_grads = total(exchange_direct(norm_grads, "ctx"))

    return (
        output[None],
        grad_inputs[None],
        grad_encoder[None],
        norm_grads[:4],
        norm_grads[4:],
        dfive[0],
        dfive[1],
        dfive[2],
        grad_w_out,
        grad_w_cq,
        dfive[3],
        dfive[4],
        grad_w_co,
        grad_inner,
        grad_outer,
    )


def solution(mesh):
    tokens = P("fsdp", "ctx", None)
    norms = P(None, ("fsdp", "ctx"))
    by_rows = P(("fsdp", "ctx"), "tp")
    by_cols = P("tp", ("fsdp", "ctx"))
    return jax.shard_map(
        body,
        mesh=mesh,
        in_specs=(
            tokens,
            tokens,
            P("fsdp"),
            P("fsdp"),
            tokens,
            norms,
            norms,
            by_rows,
            by_rows,
            by_rows,
            by_cols,
            by_rows,
            by_rows,
            by_rows,
            by_cols,
            by_rows,
            by_cols,
        ),
        out_specs=(
            tokens,
            tokens,
            tokens,
            norms,
            norms,
            by_rows,
            by_rows,
            by_rows,
            by_cols,
            by_rows,
            by_rows,
            by_rows,
            by_cols,
            by_rows,
            by_cols,
        ),
        check_vma=False,
    )
```

time: 2410 us -> 581 us (0.24)
  waiting for transfers between devices: 1890 us -> 199 us
  matrix products: 243 us -> 40.6 us
  starting transfers between devices: 2.42 us -> 176 us
  blocking collectives: 107 us -> 0 us
  Pallas kernels: 0 us -> 34.4 us
    reduce_scatter x10 -> x0, waiting for transfers between devices: 1010 us -> none  [the longest x1 183 us: return_grads(): lax.psum_scatter(grads[10], ('fsdp', 'ctx'), scatter_dimension=0, tiled=T...]
    all_gather x12 -> x0, waiting for transfers between devices: 501 us -> none  [the longest x1 75.7 us: fetch_weights(): lax.all_gather(shards[10], ('fsdp', 'ctx'), axis=0, tiled=True)]
    unnamed x40 -> x0, waiting for transfers between devices: 275 us -> none
    dot_general x72 -> x21, matrix products: 243 us -> 40.6 us  [the longest x7 14.9 us: nn(): return jnp.dot(left, right, preferred_element_type=F32)]
    ppermute x0 -> x115, waiting for transfers between devices: none -> 199 us  [the longest x69 98 us: shift(): return lax.ppermute(value, axis, [(i, (i + step) % n) for i in range(n)])]
    ppermute x0 -> x115, starting transfers between devices: none -> 176 us  [the longest x69 100 us: shift(): return lax.ppermute(value, axis, [(i, (i + step) % n) for i in range(n)])]
    all_gather x4 -> x0, blocking collectives: 107 us -> none  [the longest x1 42.7 us: fetch_weights(): lax.all_gather(shards[0], ('fsdp', 'ctx'), axis=1, tiled=True)]
    psum x6 -> x0, waiting for transfers between devices: 102 us -> none  [the longest x2 44.7 us: input_total(): return lax.psum(partial_sum, 'tp')]
  transfers between devices with their start and end apart: 34 -> 115, of which waited for: 31 -> 36; matrix products, arithmetic and copies ran while one was open for 12% -> 21% of each run, Pallas kernels for 0% -> 6%
where the time goes in v1:
time: 581 us; the launch traced here: 571 us
  waiting for transfers between devices  199 us (34%)
  starting transfers between devices  176 us (30%)
  other arithmetic  70.4 us (12%)
  local copies, waits for them, and re-layouts  44.9 us (8%)
  matrix products  40.6 us (7%)
  Pallas kernels  34.4 us (6%)
    ppermute x69, starting transfers between devices, shift(): return lax.ppermute(value, axis, [(i, (i + step) % n) for i in range(n)])  100 us
    ppermute x69, waiting for transfers between devices, shift(): return lax.ppermute(value, axis, [(i, (i + step) % n) for i in range(n)])  98 us
    ppermute x15, waiting for transfers between devices, gather_line(): lax.ppermute(downs[-1], axis, [(i, i - 1) for i in range(1, n - s + 1)])  44.7 us
    ppermute x8, waiting for transfers between devices, gather_double(): other = lax.ppermute(held, axis, [(i, i ^ 1 << bit) for i in range(n)])  35.2 us
    ppermute x15, starting transfers between devices, gather_line(): lax.ppermute(ups[-1], axis, [(i, i + 1) for i in range(s - 1, n - 1)])  26.3 us
    ppermute x8, waiting for transfers between devices, scatter_double(): came = lax.ppermute(away, axis, [(i, i ^ 1 << bit) for i in range(n)])  21.4 us
    ppermute x8, starting transfers between devices, gather_double(): other = lax.ppermute(held, axis, [(i, i ^ 1 << bit) for i in range(n)])  19.8 us
    ppermute x15, starting transfers between devices, gather_line(): lax.ppermute(downs[-1], axis, [(i, i - 1) for i in range(1, n - s + 1)])  19.5 us
  transfers between devices with their start and end apart: 115, of which 36 were waited for; matrix products, arithmetic and copies ran while one was open for 21% of the time, Pallas kernels for 6%

profile of v1, /device:TPU:0, one launch (start us, length us, event | category | flops | bytes accessed | tf_op | source)
XLA Modules:
  0.0 571.2 jit_solution(8497919407740818397)
XLA Ops:
  1.5 4.1 collective-permute-start.1
  26.8 4.4 collective-permute-start.22
  38.7 4.6 collective-permute-start.31
  46.6 5.7 %collective-permute-done.24 = bf16[64,512]{1,0:T(8,128)(2,1)S(1)} collective-permute-done((bf16[64,512]{1,0:T(8,128)(2,1)S(1)}, bf16[64,512]{1,0:T(8,128)(2,1)S(1)}, u32[]{:S(2)}, u32[]{:S(2)}) %collective-permute-start.24) | collective-permute-done | bytes 65568 | tf_op jit(solution)/shard_map/ppermute | solution.py:79
  54.4 4.6 collective-permute-start.55
  61.2 6.2 %collective-permute-done.33 = bf16[64,1024]{1,0:T(8,128)(2,1)S(1)} collective-permute-done((bf16[64,1024]{1,0:T(8,128)(2,1)S(1)}, bf16[64,1024]{1,0:T(8,128)(2,1)S(1)}, u32[]{:S(2)}, u32[]{:S(2)}) %collective-permute-start.33) | collective-permute-done | bytes 131104 | tf_op jit(solution)/shard_map/ppermute | solution.py:79
  70.8 9.4 %collective-permute-done.34 = bf16[64,1024]{1,0:T(8,128)(2,1)S(1)} collective-permute-done((bf16[64,1024]{1,0:T(8,128)(2,1)S(1)}, bf16[64,1024]{1,0:T(8,128)(2,1)S(1)}, u32[]{:S(2)}, u32[]{:S(2)}) %collective-permute-start.34) | collective-permute-done | bytes 131104 | tf_op jit(solution)/shard_map/ppermute | solution.py:79
  86.2 11.7 %collective-permute-done.17 = bf16[256,640]{1,0:T(8,128)(2,1)S(1)} collective-permute-done((bf16[256,640]{1,0:T(8,128)(2,1)S(1)}, bf16[256,640]{1,0:T(8,128)(2,1)S(1)}, u32[]{:S(2)}, u32[]{:S(2)}) %collective-permute-start.17) | collective-permute-done | bytes 327712 | tf_op jit(solution)/shard_map/ppermute | solution.py:55
  103.1 4.5 collective-permute-done.57
  107.6 4.1 collective-permute-start.44
  121.7 4.6 collective-permute-start.6
  131.5 4.4 collective-permute-done.7
  135.9 4.2 collective-permute-start.29
  142.5 4.4 collective-permute-start.53
  154.0 9.4 %collective-permute-done.9 = bf16[256,1024]{1,0:T(8,128)(2,1)S(1)} collective-permute-done((bf16[256,1024]{1,0:T(8,128)(2,1)S(1)}, bf16[256,1024]{1,0:T(8,128)(2,1)S(1)}, u32[]{:S(2)}, u32[]{:S(2)}) %collective-permute-start.9) | collective-permute-done | bytes 524320 | tf_op jit(solution)/shard_map/ppermute | solution.py:79
  163.9 7.0 %collective-permute-done.53 = bf16[1,1,256,2048]{3,2,1,0:T(8,128)(2,1)S(1)} collective-permute-done((bf16[1,1,256,2048]{3,2,1,0:T(8,128)(2,1)S(1)}, bf16[1,1,256,2048]{3,2,1,0:T(8,128)(2,1)S(1)}, u32[]{:S(2)}, u32[]{:S(2)}) %collective-permute-start.53) | collective-permute-done | bytes 1048608 | tf_op jit(solution)/shard_map/ppermute | solution.py:112
  179.0 10.5 %self_forward.1 = (bf16[2048,128]{1,0:T(8,128)(2,1)S(1)}, f32[2,2048]{1,0:T(2,128)S(1)}) custom-call(s32[3]{0:T(128)S(1)} %add_add_fusion.3.info, bf16[2048,384]{1,0:T(8,128)(2,1)S(1)} %convolution_convert_fusion.3.qkv), custom_call_target="tpu_custom_call" | custom-call | flops 2147483648 | bytes 2097152 | tf_op jit(solution)/shard_map/self_forward/pallas_call | solution.py:369
  198.3 5.1 collective-permute-start.62
  206.2 28.1 %collective-permute-done.54 = bf16[1,2,256,2048]{3,2,1,0:T(8,128)(2,1)} collective-permute-done((bf16[1,2,256,2048]{3,2,1,0:T(8,128)(2,1)}, bf16[1,2,256,2048]{3,2,1,0:T(8,128)(2,1)}, u32[]{:S(2)}, u32[]{:S(2)}) %collective-permute-start.54) | collective-permute-done | bytes 2097184 | tf_op jit(solution)/shard_map/ppermute | solution.py:112
  238.1 4.6 cross_forward.1
  264.2 7.5 %fusion.3 = bf16[512,2048]{1,0:T(8,128)(2,1)S(1)} fusion(f32[512,2048]{1,0:T(8,128)S(1)} %copy-done.77, bf16[1024,2048]{1,0:T(8,128)(2,1)S(1)} %bitcast.355, f32[512,1024]{1,0:T(8,128)S(1)} %get-tuple-element.45, bf16[1,512,1024]{2,1,0:T(8,128)(2,1)S(1)} %copy-done.25, f32[512]{0:T(512)S(1)} %broadcast_multiply_fusion.4, ...), kind=kOutput, calls=%fused_computation.7 | convolution fusion | flops 2177892352 | bytes 13645824 | tf_op jit(solution)/shard_map/dot_general | solution.py:21
  290.7 4.6 cross_backward.1
  312.8 4.0 copy.101
  334.5 15.2 %collective-permute-done.100 = bf16[2,1,256,1024]{3,2,1,0:T(8,128)(2,1)} collective-permute-done((bf16[2,1,256,1024]{3,2,1,0:T(8,128)(2,1)}, bf16[2,1,256,1024]{3,2,1,0:T(8,128)(2,1)}, u32[]{:S(2)}, u32[]{:S(2)}) %collective-permute-start.100) | collective-permute-done | bytes 1048608 | tf_op jit(solution)/shard_map/ppermute | solution.py:132
  383.2 14.7 %self_backward.1 = bf16[2048,384]{1,0:T(8,128)(2,1)S(1)} custom-call(s32[3]{0:T(128)S(1)} %add_add_fusion.3.info, bf16[2048,384]{1,0:T(8,128)(2,1)S(1)} %copy-done.1, bf16[2048,128]{1,0:T(8,128)(2,1)S(1)} %get-tuple-element.21.mixed, bf16[2048,128]{1,0:T(8,128)(2,1)S(1)} %pad_maximum_fusion.15.grad, f32[2,2048]{1,0:T(2,128)S(1)} %get-tuple-element.25.logs), custom_call_target="tpu_custom_call" | custom-call | flops 5368709120 | bytes 5242880 | tf_op jit(solution)/shard_map/self_backward/pallas_call | solution.py:394
  402.8 6.3 %collective-permute-start.89 = (bf16[256,640]{1,0:T(8,128)(2,1)S(1)}, bf16[256,640]{1,0:T(8,128)(2,1)S(1)}, u32[]{:S(2)}, u32[]{:S(2)}) collective-permute-start(bf16[256,640]{1,0:T(8,128)(2,1)S(1)} %get-tuple-element.87), channel_id=1, source_target_pairs={{0,8},{8,16},{16,24},{24,0},{1,9},{9,17},{17,25},{25,1},{2,10},{10... | collective-permute-start | bytes 983048 | tf_op jit(solution)/shard_map/ppermute | solution.py:55
  449.2 4.8 collective-permute-done.103
  477.8 19.9 %collective-permute-start.71 = (bf16[256,1024]{1,0:T(8,128)(2,1)S(1)}, bf16[256,1024]{1,0:T(8,128)(2,1)S(1)}, u32[]{:S(2)}, u32[]{:S(2)}) collective-permute-start(bf16[256,1024]{1,0:T(8,128)(2,1)S(1)} %get-tuple-element.80), channel_id=1, source_target_pairs={{0,4},{2,6},{4,0},{6,2},{1,5},{3,7},{5,1},{7,3},{8,12},{10,14},{12... | collective-permute-start | bytes 1572872 | tf_op jit(solution)/shard_map/ppermute | solution.py:55
  497.9 6.4 %collective-permute-start.109 = (bf16[64,2048]{1,0:T(8,128)(2,1)S(1)}, bf16[64,2048]{1,0:T(8,128)(2,1)}, u32[]{:S(2)}, u32[]{:S(2)}) collective-permute-start(bf16[64,2048]{1,0:T(8,128)(2,1)S(1)} %get-tuple-element.99), channel_id=1, source_target_pairs={{0,6},{2,0},{4,2},{6,4},{1,7},{3,1},{5,3},{7,5},{8,14},{10,8},{12,... | collective-permute-start | bytes 786440 | tf_op jit(solution)/shard_map/ppermute | solution.py:55
  505.2 4.9 collective-permute-done.72
  510.1 30.3 %collective-permute-done.71 = bf16[256,1024]{1,0:T(8,128)(2,1)S(1)} collective-permute-done((bf16[256,1024]{1,0:T(8,128)(2,1)S(1)}, bf16[256,1024]{1,0:T(8,128)(2,1)S(1)}, u32[]{:S(2)}, u32[]{:S(2)}) %collective-permute-start.71) | collective-permute-done | bytes 524320 | tf_op jit(solution)/shard_map/ppermute | solution.py:55
  555.9 9.2 %collective-permute-done.108 = bf16[64,2048]{1,0:T(8,128)(2,1)S(1)} collective-permute-done((bf16[64,2048]{1,0:T(8,128)(2,1)S(1)}, bf16[64,2048]{1,0:T(8,128)(2,1)S(1)}, u32[]{:S(2)}, u32[]{:S(2)}) %collective-permute-start.108) | collective-permute-done | bytes 262176 | tf_op jit(solution)/shard_map/ppermute | solution.py:55
  (564 shorter events, 297.1 us)
Async XLA Ops:
  8.4 25.5 %collective-permute-start.40 = (bf16[32,1024]{1,0:T(8,128)(2,1)S(1)}, bf16[32,1024]{1,0:T(8,128)(2,1)S(1)}, u32[]{:S(2)}, u32[]{:S(2)}) collective-permute-start(bf16[32,1024]{1,0:T(8,128)(2,1)S(1)} %dynamic-slice_bitcast_fusion.21), channel_id=1, source_target_pairs={{0,4},{2,6},{4,0},{6,2},{1,5},{3,7},{5,1},{7,3},{8,12},{10,14},{12... | collective-permute-start | bytes 196616 | tf_op jit(solution)/shard_map/ppermute | solution.py:55
  9.4 25.8 %collective-permute-start.41 = (bf16[32,1024]{1,0:T(8,128)(2,1)S(1)}, bf16[32,1024]{1,0:T(8,128)(2,1)S(1)}, u32[]{:S(2)}, u32[]{:S(2)}) collective-permute-start(bf16[32,1024]{1,0:T(8,128)(2,1)S(1)} %dynamic-slice_bitcast_fusion.21), channel_id=1, source_target_pairs={{0,6},{2,0},{4,2},{6,4},{1,7},{3,1},{5,3},{7,5},{8,14},{10,8},{12,... | collective-permute-start | bytes 196616 | tf_op jit(solution)/shard_map/ppermute | solution.py:55
  38.7 20.3 %collective-permute-start.31 = (bf16[64,1024]{1,0:T(8,128)(2,1)S(1)}, bf16[64,1024]{1,0:T(8,128)(2,1)S(1)}, u32[]{:S(2)}, u32[]{:S(2)}) collective-permute-start(bf16[64,1024]{1,0:T(8,128)(2,1)S(1)} %pad_maximum_fusion.18), channel_id=1, source_target_pairs={{0,2},{2,4},{4,6},{1,3},{3,5},{5,7},{8,10},{10,12},{12,14},{9,11},... | collective-permute-start | bytes 393224 | tf_op jit(solution)/shard_map/ppermute | solution.py:78
  43.3 39.5 %collective-permute-start.56 = (bf16[64,2048]{1,0:T(8,128)(2,1)S(1)}, bf16[64,2048]{1,0:T(8,128)(2,1)S(1)}, u32[]{:S(2)}, u32[]{:S(2)}) collective-permute-start(bf16[64,2048]{1,0:T(8,128)(2,1)S(1)} %bitcast.373), channel_id=1, source_target_pairs={{2,0},{4,2},{6,4},{3,1},{5,3},{7,5},{10,8},{12,10},{14,12},{11,9},... | collective-permute-start | bytes 786440 | tf_op jit(solution)/shard_map/ppermute | solution.py:79
  54.4 28.7 %collective-permute-start.55 = (bf16[64,2048]{1,0:T(8,128)(2,1)S(1)}, bf16[64,2048]{1,0:T(8,128)(2,1)S(1)}, u32[]{:S(2)}, u32[]{:S(2)}) collective-permute-start(bf16[64,2048]{1,0:T(8,128)(2,1)S(1)} %bitcast.374), channel_id=1, source_target_pairs={{0,2},{2,4},{4,6},{1,3},{3,5},{5,7},{8,10},{10,12},{12,14},{9,11},... | collective-permute-start | bytes 786440 | tf_op jit(solution)/shard_map/ppermute | solution.py:78
  102.5 23.9 %collective-permute-start.51 = (bf16[64,2048]{1,0:T(8,128)(2,1)S(1)}, bf16[64,2048]{1,0:T(8,128)(2,1)S(1)}, u32[]{:S(2)}, u32[]{:S(2)}) collective-permute-start(bf16[64,2048]{1,0:T(8,128)(2,1)S(1)} %collective-permute-done.47), channel_id=1, source_target_pairs={{2,4},{4,6},{3,5},{5,7},{10,12},{12,14},{11,13},{13,15},{18,20},{2... | collective-permute-start | bytes 786440 | tf_op jit(solution)/shard_map/ppermute | solution.py:78
  126.4 20.6 %collective-permute-start.37 = (bf16[1,1,256,1024]{3,2,1,0:T(8,128)(2,1)S(1)}, bf16[1,1,256,1024]{3,2,1,0:T(8,128)(2,1)S(1)}, u32[]{:S(2)}, u32[]{:S(2)}) collective-permute-start(bf16[1,1,256,1024]{3,2,1,0:T(8,128)(2,1)S(1)} %maximum_bitcast_fusion.3), channel_id=1, source_target_pairs={{0,8},{8,0},{16,24},{24,16},{1,9},{9,1},{17,25},{25,17},{2,10},{10... | collective-permute-start | bytes 1572872 | tf_op jit(solution)/shard_map/ppermute | solution.py:112
  135.9 27.8 %collective-permute-start.29 = (bf16[2,1,256,512]{3,2,1,0:T(8,128)(2,1)S(1)}, bf16[2,1,256,512]{3,2,1,0:T(8,128)(2,1)S(1)}, u32[]{:S(2)}, u32[]{:S(2)}) collective-permute-start(bf16[2,1,256,512]{3,2,1,0:T(8,128)(2,1)S(1)} %pad_maximum_fusion.12), channel_id=1, source_target_pairs={{0,8},{8,0},{16,24},{24,16},{1,9},{9,1},{17,25},{25,17},{2,10},{10... | collective-permute-start | bytes 1572872 | tf_op jit(solution)/shard_map/ppermute | solution.py:112
  142.5 28.4 %collective-permute-start.53 = (bf16[1,1,256,2048]{3,2,1,0:T(8,128)(2,1)S(1)}, bf16[1,1,256,2048]{3,2,1,0:T(8,128)(2,1)S(1)}, u32[]{:S(2)}, u32[]{:S(2)}) collective-permute-start(bf16[1,1,256,2048]{3,2,1,0:T(8,128)(2,1)S(1)} %maximum_bitcast_fusion.1), channel_id=1, source_target_pairs={{0,8},{8,0},{16,24},{24,16},{1,9},{9,1},{17,25},{25,17},{2,10},{10... | collective-permute-start | bytes 3145736 | tf_op jit(solution)/shard_map/ppermute | solution.py:112
  147.0 26.8 %collective-permute-start.61 = (bf16[1,1,256,2048]{3,2,1,0:T(8,128)(2,1)S(1)}, bf16[1,1,256,2048]{3,2,1,0:T(8,128)(2,1)S(1)}, u32[]{:S(2)}, u32[]{:S(2)}) collective-permute-start(bf16[1,1,256,2048]{3,2,1,0:T(8,128)(2,1)S(1)} %maximum_bitcast_fusion.2), channel_id=1, source_target_pairs={{0,16},{8,24},{16,0},{24,8},{1,17},{9,25},{17,1},{25,9},{2,18},{10... | collective-permute-start | bytes 3145736 | tf_op jit(solution)/shard_map/ppermute | solution.py:112
  153.8 50.6 %collective-permute-start.38 = (bf16[1,2,256,1024]{3,2,1,0:T(8,128)(2,1)}, bf16[1,2,256,1024]{3,2,1,0:T(8,128)(2,1)}, u32[]{:S(2)}, u32[]{:S(2)}) collective-permute-start(bf16[1,2,256,1024]{3,2,1,0:T(8,128)(2,1)} %pad_maximum_fusion.9), channel_id=1, source_target_pairs={{0,16},{8,24},{16,0},{24,8},{1,17},{9,25},{17,1},{25,9},{2,18},{10... | collective-permute-start | bytes 3145736 | tf_op jit(solution)/shard_map/ppermute | solution.py:112
  173.0 61.3 %collective-permute-start.54 = (bf16[1,2,256,2048]{3,2,1,0:T(8,128)(2,1)}, bf16[1,2,256,2048]{3,2,1,0:T(8,128)(2,1)}, u32[]{:S(2)}, u32[]{:S(2)}) collective-permute-start(bf16[1,2,256,2048]{3,2,1,0:T(8,128)(2,1)} %pad_maximum_fusion.3), channel_id=1, source_target_pairs={{0,16},{8,24},{16,0},{24,8},{1,17},{9,25},{17,1},{25,9},{2,18},{10... | collective-permute-start | bytes 6291464 | tf_op jit(solution)/shard_map/ppermute | solution.py:112
  198.3 45.6 %collective-permute-start.62 = (bf16[2,1,256,2048]{3,2,1,0:T(8,128)(2,1)}, bf16[2,1,256,2048]{3,2,1,0:T(8,128)(2,1)}, u32[]{:S(2)}, u32[]{:S(2)}) collective-permute-start(bf16[2,1,256,2048]{3,2,1,0:T(8,128)(2,1)} %pad_maximum_fusion.4), channel_id=1, source_target_pairs={{0,8},{8,0},{16,24},{24,16},{1,9},{9,1},{17,25},{25,17},{2,10},{10... | collective-permute-start | bytes 6291464 | tf_op jit(solution)/shard_map/ppermute | solution.py:112
  204.4 32.1 %collective-permute-start.30 = (bf16[512,1024]{1,0:T(8,128)(2,1)S(1)}, bf16[512,1024]{1,0:T(8,128)(2,1)S(1)}, u32[]{:S(2)}, u32[]{:S(2)}) collective-permute-start(bf16[512,1024]{1,0:T(8,128)(2,1)S(1)} %convolution_convert_fusion.9), channel_id=1, source_target_pairs={{0,1},{1,0},{2,3},{3,2},{4,5},{5,4},{6,7},{7,6},{8,9},{9,8},{10,11... | collective-permute-start | bytes 3145736 | tf_op jit(solution)/shard_map/ppermute | solution.py:55
  279.2 90.9 %collective-permute-start.110 = (bf16[2,1,256,2048]{3,2,1,0:T(8,128)(2,1)}, bf16[2,1,256,2048]{3,2,1,0:T(8,128)(2,1)}, u32[]{:S(2)}, u32[]{:S(2)}) collective-permute-start(bf16[2,1,256,2048]{3,2,1,0:T(8,128)(2,1)} %constant_dynamic-slice_fusion.1), channel_id=1, source_target_pairs={{0,8},{8,0},{16,24},{24,16},{1,9},{9,1},{17,25},{25,17},{2,10},{10... | collective-permute-start | bytes 6291464 | tf_op jit(solution)/shard_map/ppermute | solution.py:132
  319.2 30.5 %collective-permute-start.100 = (bf16[2,1,256,1024]{3,2,1,0:T(8,128)(2,1)}, bf16[2,1,256,1024]{3,2,1,0:T(8,128)(2,1)}, u32[]{:S(2)}, u32[]{:S(2)}) collective-permute-start(bf16[2,1,256,1024]{3,2,1,0:T(8,128)(2,1)} %constant_dynamic-slice_fusion.5), channel_id=1, source_target_pairs={{0,8},{8,0},{16,24},{24,16},{1,9},{9,1},{17,25},{25,17},{2,10},{10... | collective-permute-start | bytes 3145736 | tf_op jit(solution)/shard_map/ppermute | solution.py:132
  328.3 48.9 %collective-permute-start.105 = (bf16[1,2,256,2048]{3,2,1,0:T(8,128)(2,1)}, bf16[1,2,256,2048]{3,2,1,0:T(8,128)(2,1)}, u32[]{:S(2)}, u32[]{:S(2)}) collective-permute-start(bf16[1,2,256,2048]{3,2,1,0:T(8,128)(2,1)} %constant_dynamic-slice_fusion.3), channel_id=1, source_target_pairs={{0,16},{8,24},{16,0},{24,8},{1,17},{9,25},{17,1},{25,9},{2,18},{10... | collective-permute-start | bytes 6291464 | tf_op jit(solution)/shard_map/ppermute | solution.py:132
  329.3 25.0 %collective-permute-start.65 = (bf16[512,1024]{1,0:T(8,128)(2,1)}, bf16[512,1024]{1,0:T(8,128)(2,1)}, u32[]{:S(2)}, u32[]{:S(2)}) collective-permute-start(bf16[512,1024]{1,0:T(8,128)(2,1)} %convolution_convert_fusion.7), channel_id=1, source_target_pairs={{0,1},{1,0},{2,3},{3,2},{4,5},{5,4},{6,7},{7,6},{8,9},{9,8},{10,11... | collective-permute-start | bytes 3145736 | tf_op jit(solution)/shard_map/ppermute | solution.py:55
  353.1 69.5 %collective-permute-start.101 = (bf16[1,1,256,1024]{3,2,1,0:T(8,128)(2,1)}, bf16[1,1,256,1024]{3,2,1,0:T(8,128)(2,1)}, u32[]{:S(2)}, u32[]{:S(2)}) collective-permute-start(bf16[1,1,256,1024]{3,2,1,0:T(8,128)(2,1)} %constant_dynamic-slice_fusion.4), channel_id=1, source_target_pairs={{0,16},{8,24},{16,0},{24,8},{1,17},{9,25},{17,1},{25,9},{2,18},{10... | collective-permute-start | bytes 1572872 | tf_op jit(solution)/shard_map/ppermute | solution.py:132
  377.2 49.8 %collective-permute-start.95 = (bf16[1,2,256,512]{3,2,1,0:T(8,128)(2,1)S(1)}, bf16[1,2,256,512]{3,2,1,0:T(8,128)(2,1)S(1)}, u32[]{:S(2)}, u32[]{:S(2)}) collective-permute-start(bf16[1,2,256,512]{3,2,1,0:T(8,128)(2,1)S(1)} %constant_dynamic-slice_fusion.7), channel_id=1, source_target_pairs={{0,16},{8,24},{16,0},{24,8},{1,17},{9,25},{17,1},{25,9},{2,18},{10... | collective-permute-start | bytes 1572872 | tf_op jit(solution)/shard_map/ppermute | solution.py:132
  415.0 48.3 %collective-permute-start.111 = (bf16[1,1,256,2048]{3,2,1,0:T(8,128)(2,1)}, bf16[1,1,256,2048]{3,2,1,0:T(8,128)(2,1)}, u32[]{:S(2)}, u32[]{:S(2)}) collective-permute-start(bf16[1,1,256,2048]{3,2,1,0:T(8,128)(2,1)} %constant_dynamic-slice_fusion), channel_id=1, source_target_pairs={{0,16},{8,24},{16,0},{24,8},{1,17},{9,25},{17,1},{25,9},{2,18},{10... | collective-permute-start | bytes 3145736 | tf_op jit(solution)/shard_map/ppermute | solution.py:132
  420.5 52.1 %collective-permute-start.69 = (bf16[4,256,1024]{2,1,0:T(8,128)(2,1)}, bf16[4,256,1024]{2,1,0:T(8,128)(2,1)}, u32[]{:S(2)}, u32[]{:S(2)}) collective-permute-start(bf16[4,256,1024]{2,1,0:T(8,128)(2,1)} %slice_bitcast_fusion), channel_id=1, source_target_pairs={{0,1},{1,0},{2,3},{3,2},{4,5},{5,4},{6,7},{7,6},{8,9},{9,8},{10,11... | collective-permute-start | bytes 6291464 | tf_op jit(solution)/shard_map/ppermute | solution.py:55
  428.6 20.1 %collective-permute-start.102 = (bf16[64,1024]{1,0:T(8,128)(2,1)}, bf16[64,1024]{1,0:T(8,128)(2,1)}, u32[]{:S(2)}, u32[]{:S(2)}) collective-permute-start(bf16[64,1024]{1,0:T(8,128)(2,1)} %get-tuple-element.128), channel_id=1, source_target_pairs={{0,2},{2,4},{4,6},{6,0},{1,3},{3,5},{5,7},{7,1},{8,10},{10,12},{12... | collective-permute-start | bytes 393224 | tf_op jit(solution)/shard_map/ppermute | solution.py:55
  428.6 20.2 %collective-permute-start.104 = (bf16[64,1024]{1,0:T(8,128)(2,1)}, bf16[64,1024]{1,0:T(8,128)(2,1)}, u32[]{:S(2)}, u32[]{:S(2)}) collective-permute-start(bf16[64,1024]{1,0:T(8,128)(2,1)} %get-tuple-element.129), channel_id=1, source_target_pairs={{0,6},{2,0},{4,2},{6,4},{1,7},{3,1},{5,3},{7,5},{8,14},{10,8},{12,... | collective-permute-start | bytes 393224 | tf_op jit(solution)/shard_map/ppermute | solution.py:55
  448.7 23.4 %collective-permute-start.106 = (bf16[1,1,256,2048]{3,2,1,0:T(8,128)(2,1)S(1)}, bf16[1,1,256,2048]{3,2,1,0:T(8,128)(2,1)S(1)}, u32[]{:S(2)}, u32[]{:S(2)}) collective-permute-start(bf16[1,1,256,2048]{3,2,1,0:T(8,128)(2,1)S(1)} %copy-done.45), channel_id=1, source_target_pairs={{0,8},{8,0},{16,24},{24,16},{1,9},{9,1},{17,25},{25,17},{2,10},{10... | collective-permute-start | bytes 3145736 | tf_op jit(solution)/shard_map/ppermute | solution.py:132
  465.2 32.6 %collective-permute-start.114 = (bf16[64,2048]{1,0:T(8,128)(2,1)S(1)}, bf16[64,2048]{1,0:T(8,128)(2,1)S(1)}, u32[]{:S(2)}, u32[]{:S(2)}) collective-permute-start(bf16[64,2048]{1,0:T(8,128)(2,1)S(1)} %get-tuple-element.96), channel_id=1, source_target_pairs={{0,6},{2,0},{4,2},{6,4},{1,7},{3,1},{5,3},{7,5},{8,14},{10,8},{12,... | collective-permute-start | bytes 786440 | tf_op jit(solution)/shard_map/ppermute | solution.py:55
  469.0 28.8 %collective-permute-start.113 = (bf16[64,2048]{1,0:T(8,128)(2,1)S(1)}, bf16[64,2048]{1,0:T(8,128)(2,1)S(1)}, u32[]{:S(2)}, u32[]{:S(2)}) collective-permute-start(bf16[64,2048]{1,0:T(8,128)(2,1)S(1)} %get-tuple-element.97), channel_id=1, source_target_pairs={{0,4},{2,6},{4,0},{6,2},{1,5},{3,7},{5,1},{7,3},{8,12},{10,14},{12... | collective-permute-start | bytes 786440 | tf_op jit(solution)/shard_map/ppermute | solution.py:55
  475.7 29.5 %collective-permute-start.70 = (bf16[256,1024]{1,0:T(8,128)(2,1)S(1)}, bf16[256,1024]{1,0:T(8,128)(2,1)S(1)}, u32[]{:S(2)}, u32[]{:S(2)}) collective-permute-start(bf16[256,1024]{1,0:T(8,128)(2,1)S(1)} %get-tuple-element.78), channel_id=1, source_target_pairs={{0,6},{2,0},{4,2},{6,4},{1,7},{3,1},{5,3},{7,5},{8,14},{10,8},{12,... | collective-permute-start | bytes 1572872 | tf_op jit(solution)/shard_map/ppermute | solution.py:55
  476.6 33.5 %collective-permute-start.72 = (bf16[256,1024]{1,0:T(8,128)(2,1)S(1)}, bf16[256,1024]{1,0:T(8,128)(2,1)S(1)}, u32[]{:S(2)}, u32[]{:S(2)}) collective-permute-start(bf16[256,1024]{1,0:T(8,128)(2,1)S(1)} %get-tuple-element.79), channel_id=1, source_target_pairs={{0,2},{2,4},{4,6},{6,0},{1,3},{3,5},{5,7},{7,1},{8,10},{10,12},{12... | collective-permute-start | bytes 1572872 | tf_op jit(solution)/shard_map/ppermute | solution.py:55
  477.8 62.6 %collective-permute-start.71 = (bf16[256,1024]{1,0:T(8,128)(2,1)S(1)}, bf16[256,1024]{1,0:T(8,128)(2,1)S(1)}, u32[]{:S(2)}, u32[]{:S(2)}) collective-permute-start(bf16[256,1024]{1,0:T(8,128)(2,1)S(1)} %get-tuple-element.80), channel_id=1, source_target_pairs={{0,4},{2,6},{4,0},{6,2},{1,5},{3,7},{5,1},{7,3},{8,12},{10,14},{12... | collective-permute-start | bytes 1572872 | tf_op jit(solution)/shard_map/ppermute | solution.py:55
  497.8 55.9 %collective-permute-start.107 = (bf16[64,2048]{1,0:T(8,128)(2,1)S(1)}, bf16[64,2048]{1,0:T(8,128)(2,1)}, u32[]{:S(2)}, u32[]{:S(2)}) collective-permute-start(bf16[64,2048]{1,0:T(8,128)(2,1)S(1)} %get-tuple-element.98), channel_id=1, source_target_pairs={{0,2},{2,4},{4,6},{6,0},{1,3},{3,5},{5,7},{7,1},{8,10},{10,12},{12... | collective-permute-start | bytes 786440 | tf_op jit(solution)/shard_map/ppermute | solution.py:55
  497.9 56.4 %collective-permute-start.109 = (bf16[64,2048]{1,0:T(8,128)(2,1)S(1)}, bf16[64,2048]{1,0:T(8,128)(2,1)}, u32[]{:S(2)}, u32[]{:S(2)}) collective-permute-start(bf16[64,2048]{1,0:T(8,128)(2,1)S(1)} %get-tuple-element.99), channel_id=1, source_target_pairs={{0,6},{2,0},{4,2},{6,4},{1,7},{3,1},{5,3},{7,5},{8,14},{10,8},{12,... | collective-permute-start | bytes 786440 | tf_op jit(solution)/shard_map/ppermute | solution.py:55
  (161 other events, 1833.4 us)

commit v2 on v1

--- a/solution.py
+++ b/solution.py
@@ -50,51 +50,17 @@
     return (grad_input, jnp.sum(grad_result * normed, axis=0), jnp.sum(grad_result, axis=0))
 
 
-def shift(value, axis, step):
+def flip(value, axis, mask):
     n = lax.axis_size(axis)
-    return lax.ppermute(value, axis, [(i, (i + step) % n) for i in range(n)])
+    return lax.ppermute(value, axis, [(i, i ^ mask) for i in range(n)])
 
 
 def swap(value):
-    return shift(value, "tp", 1)
-
-
-def in_order(pieces, axis):
-    n = len(pieces)
-    me = lax.axis_index(axis)
-    return [lax.select_n(me, *[pieces[(m - j) % n] for m in range(n)]) for j in range(n)]
-
-
-def gather_direct(value, axis):
-    n = lax.axis_size(axis)
-    return [value] + [shift(value, axis, s) for s in range(1, n)]
-
-
-def gather_line(value, axis):
-    n = lax.axis_size(axis)
-    me = lax.axis_index(axis)
-    ups, downs = [value], [value]
-    for s in range(1, n):
-        ups.append(lax.ppermute(ups[-1], axis, [(i, i + 1) for i in range(s - 1, n - 1)]))
-        downs.append(lax.ppermute(downs[-1], axis, [(i, i - 1) for i in range(1, n - s + 1)]))
-    return [value] + [jnp.where(me >= s, ups[s], downs[n - s]) for s in range(1, n)]
-
-
-def exchange_direct(blocks, axis):
-    n = lax.axis_size(axis)
-    me = lax.axis_index(axis)
-
-    def pick(d):
-        return lax.dynamic_index_in_dim(blocks, d, 0, keepdims=False)
-
-    return [pick(me)] + [shift(pick((me + s) % n), axis, s) for s in range(1, n)]
-
-
-def total(pieces):
-    out = pieces[0].astype(F32)
-    for piece in pieces[1:]:
-        out = out + piece.astype(F32)
-    return out
+    return flip(value, "tp", 1)
+
+
+def tie(value, *others):
+    return lax.optimization_barrier((value,) + others)[0]
 
 
 def bits_of(axis, low_first):
@@ -103,50 +69,247 @@
     return order if low_first else order[::-1]
 
 
-def gather_double(value, axis, low_first):
+def bit_at(axis, bit):
+    return (lax.axis_index(axis) >> bit) & 1
+
+
+class Gathering:
+    def __init__(self, value, axis, low_first):
+        self.axis, self.order = axis, bits_of(axis, low_first)
+        self.blocks, self.came = {0: value}, None
+
+    def start(self, *others):
+        bit = self.order[0]
+        keys = sorted(self.blocks)
+        sent = [self.blocks[k] for k in keys]
+        sent = sent[0] if len(sent) == 1 else jnp.concatenate(sent, axis=0)
+        if others:
+            sent = tie(sent, *others)
+        self.came = flip(sent, self.axis, 1 << bit)
+        return self.came
+
+    def join(self):
+        bit = self.order.pop(0)
+        mine = bit_at(self.axis, bit)
+        keys = sorted(self.blocks)
+        rows = self.came.shape[0] // len(keys)
+        blocks = {}
+        for place, k in enumerate(keys):
+            held, other = self.blocks[k], self.came[place * rows : (place + 1) * rows]
+            blocks[k] = jnp.where(mine == 0, held, other)
+            blocks[k | 1 << bit] = jnp.where(mine == 0, other, held)
+        self.blocks = blocks
+
+    def step(self, *others):
+        self.join()
+        return self.start(*others)
+
+    def end(self):
+        self.join()
+        return jnp.concatenate([self.blocks[k] for k in sorted(self.blocks)], axis=0)
+
+
+class Doubling:
+    def __init__(self, value, *others):
+        cut = value.shape[0] // 2
+        self.parts = [
+            Gathering(value[:cut], "fsdp", True),
+            Gathering(value[cut:], "fsdp", False),
+        ]
+        self.start(*others)
+
+    def start(self, *others):
+        self.came = [g.start(*others) for g in self.parts]
+
+    def after(self, *others):
+        for g in self.parts:
+            g.came = tie(g.came, *others)
+
+    def step(self, *others):
+        self.after(*others)
+        for g in self.parts:
+            g.join()
+        self.start()
+
+    def end(self, *others):
+        self.after(*others)
+        for g in self.parts:
+            g.join()
+        keys = sorted(self.parts[0].blocks)
+        return jnp.concatenate([g.blocks[k] for k in keys for g in self.parts], axis=0)
+
+
+def gather_offsets(value, axis, low_first, seen=None, late=None):
+    found = {0: value}
+    order = bits_of(axis, low_first)
+    for bit in order:
+        keys = sorted(found)
+        sent = [found[k] for k in keys]
+        sent = sent[0] if len(sent) == 1 else jnp.concatenate(sent, axis=0)
+        if late is not None and bit == order[-1]:
+            sent = tie(sent, late)
+        came = flip(sent, axis, 1 << bit)
+        rows = value.shape[0]
+        if seen is not None:
+            seen.append(came)
+        for place, k in enumerate(keys):
+            found[k ^ (1 << bit)] = came[place * rows : (place + 1) * rows]
+    return [found[k] for k in range(lax.axis_size(axis))]
+
+
+def natural(pieces, axis, dim=0):
+    n = len(pieces)
+    me = lax.axis_index(axis)
+    return jnp.concatenate(
+        [lax.select_n(me, *[pieces[j ^ m] for m in range(n)]) for j in range(n)], axis=dim
+    )
+
+
+def gather_direct(value, axis):
     n = lax.axis_size(axis)
-    count = n.bit_length() - 1
+    return natural([value] + [flip(value, axis, k) for k in range(1, n)], axis)
+
+
+def exchange_direct(blocks, axis):
     me = lax.axis_index(axis)
-    held = value.reshape((1,) * count + value.shape)
-    for bit in bits_of(axis, low_first):
-        other = lax.ppermute(held, axis, [(i, i ^ (1 << bit)) for i in range(n)])
-        mine = (me >> bit) & 1
-        held = jnp.concatenate(
-            [jnp.where(mine == 0, held, other), jnp.where(mine == 0, other, held)],
-            axis=count - 1 - bit,
-        )
-    return held.reshape((n * value.shape[0],) + value.shape[1:])
-
-
-def scatter_double(value, axis, low_first):
+    out = [lax.dynamic_index_in_dim(blocks, me ^ k, 0, keepdims=False) for k in range(len(blocks))]
+    return out[:1] + [flip(out[k], axis, k) for k in range(1, len(blocks))]
+
+
+def half_rows(held, index, bit, bits):
+    rows = held.shape[0] // 2
+    if bits[0] == bit:
+        return lax.dynamic_slice_in_dim(held, index * rows, rows, 0)
+    before = 1 << bits.index(bit)
+    view = held.reshape(before, 2, rows // before, held.shape[1])
+    return lax.dynamic_slice_in_dim(view, index, 1, 1).reshape(rows, held.shape[1])
+
+
+class Scattering:
+    def __init__(self, legs, away, held, bits, first):
+        self.legs = [(axis, bit) for axis, low in legs for bit in bits_of(axis, low)][1:]
+        self.bits = [b for b in bits if b != first]
+        self.held, self.axis = held, legs[0][0]
+        self.came = flip(away, legs[0][0], 1 << first)
+
+    def step(self):
+        axis, bit = self.legs.pop(0)
+        if axis != self.axis:
+            self.axis, self.bits = axis, bits_of(axis, False)
+        mine = bit_at(axis, bit)
+
+        def part(index):
+            held = half_rows(self.held, index, bit, self.bits).astype(F32)
+            return (held + half_rows(self.came, index, bit, self.bits).astype(F32)).astype(BF)
+
+        away, held = part(1 - mine), part(mine)
+        self.bits = [b for b in self.bits if b != bit]
+        self.came, self.held = flip(away, axis, 1 << bit), held
+
+    def end(self):
+        return self.held.astype(F32) + self.came.astype(F32)
+
+
+def scatter_value(value, legs):
+    axis, low = legs[0]
+    bit, bits = bits_of(axis, low)[0], bits_of(axis, False)
+    mine = bit_at(axis, bit)
+    return Scattering(
+        legs, half_rows(value, 1 - mine, bit, bits), half_rows(value, mine, bit, bits), bits, bit
+    )
+
+
+class Halving:
+    def __init__(self, pairs, *others):
+        n = lax.axis_size("fsdp")
+        bits = bits_of("fsdp", False)
+        firsts = [bits_of("fsdp", True)[0], bits_of("fsdp", False)[0]]
+
+        def product(flipped):
+            out = []
+            for left, right in pairs:
+                rows = left.shape[1] // n
+                cut = rows // 2
+                chosen = []
+                for place, bit in enumerate(firsts):
+                    index = bit_at("fsdp", bit) ^ flipped
+                    sides = [
+                        jnp.concatenate(
+                            [
+                                left[:, b * rows + place * cut : b * rows + (place + 1) * cut]
+                                for b in range(n)
+                                if b >> bit & 1 == v
+                            ],
+                            axis=1,
+                        )
+                        for v in range(2)
+                    ]
+                    chosen.append(jnp.where(index == 0, sides[0], sides[1]))
+                out.append(tn(jnp.concatenate(chosen, axis=1), right).astype(BF))
+            return out[0] if len(out) == 1 else jnp.concatenate(out, axis=1)
+
+        away, keep = product(1), product(0)
+        if others:
+            away = tie(away, *others)
+        cut = away.shape[0] // 2
+        self.parts = [
+            Scattering(
+                [("fsdp", low)],
+                away[place * cut : (place + 1) * cut],
+                keep[place * cut : (place + 1) * cut],
+                bits,
+                firsts[place],
+            )
+            for place, low in enumerate((True, False))
+        ]
+        self.ctx = False
+
+    def after(self, *others):
+        for p in self.parts:
+            p.came = tie(p.came, *others)
+
+    def flight(self):
+        return [p.came for p in self.parts]
+
+    def held(self):
+        return [p.held for p in self.parts]
+
+    def over(self):
+        return not self.parts[0].legs
+
+    def step(self, *others):
+        if others:
+            self.after(*others)
+        if not self.over():
+            while not self.over():
+                for p in self.parts:
+                    p.step()
+        elif not self.ctx:
+            value = jnp.concatenate([p.end().astype(BF) for p in self.parts], axis=0)
+            self.parts, self.ctx = [scatter_value(value, [("ctx", True)])], True
+
+    def end(self, *others):
+        if others:
+            self.after(*others)
+        return self.parts[0].end()
+
+
+def scatter_offsets(pieces, axis, seen=None):
     n = lax.axis_size(axis)
-    count = n.bit_length() - 1
-    me = lax.axis_index(axis)
-    rows = value.shape[0] // n
-    held = value.reshape((2,) * count + (rows,) + value.shape[1:])
-    for bit in bits_of(axis, low_first):
-        dim = count - 1 - bit
-        mine = (me >> bit) & 1
-        away = lax.dynamic_slice_in_dim(held, 1 - mine, 1, dim)
-        keep = lax.dynamic_slice_in_dim(held, mine, 1, dim)
-        came = lax.ppermute(away, axis, [(i, i ^ (1 << bit)) for i in range(n)])
-        held = (keep.astype(F32) + came.astype(F32)).astype(value.dtype)
-    return held.reshape((rows,) + value.shape[1:])
-
-
-def scatter_direct(value, axis):
-    n = lax.axis_size(axis)
-    blocks = value.reshape((n, value.shape[0] // n) + value.shape[1:])
-    return total(exchange_direct(blocks, axis))
-
-
-def fetch_rows(shard, low_first):
-    held = jnp.concatenate(in_order(gather_line(shard, "ctx"), "ctx"), axis=0)
-    return gather_double(held, "fsdp", low_first)
-
-
-def return_rows(grad, low_first):
-    return scatter_direct(scatter_double(grad, "fsdp", low_first), "ctx")
+    held = dict(enumerate(pieces))
+    for bit in bits_of(axis, True):
+        last = n == 2 << bit
+        away = [held[k].astype(BF) for k in sorted(held) if k >> bit & 1]
+        came = flip(away[0] if len(away) == 1 else jnp.concatenate(away, axis=0), axis, 1 << bit)
+        rows = pieces[0].shape[0]
+        if seen is not None:
+            seen.append(came)
+        held = {k: v for k, v in held.items() if not k >> bit & 1}
+        for place, k in enumerate(sorted(held)):
+            held[k] = held[k].astype(F32) + came[place * rows : (place + 1) * rows].astype(F32)
+            if not last:
+                held[k] = held[k].astype(BF)
+    return held[0]
 
 
 def lanes_of(head, shape):
@@ -154,9 +317,44 @@
     return (lane // HEAD_DIM) == head
 
 
-def spans(count, block):
-    half = block // 2
-    return half
+def project_kernel(x_ref, scales, weight, kept, out):
+    x = x_ref[...].astype(F32)
+    width = x.shape[1]
+    centred = x - jnp.sum(x, axis=1, keepdims=True) * (1.0 / width)
+    spread = jnp.sum(centred * centred, axis=1, keepdims=True) * (1.0 / width)
+    normed = centred * lax.rsqrt(spread + EPS)
+    attn_in = (normed * scales[0:1, :] + scales[1:2, :]).astype(BF)
+    kept[:, :width] = attn_in
+    kept[:, width:] = normed.astype(BF)
+    out[...] = nn(attn_in, weight[...]).astype(BF)
+
+
+def project(x_all, scales, weight):
+    slots, width = x_all.shape
+    cols = weight.shape[1]
+    block = min(256, slots)
+    return pl.pallas_call(
+        project_kernel,
+        grid=(slots // block,),
+        in_specs=[
+            pl.BlockSpec((block, width), lambda i: (i, 0)),
+            pl.BlockSpec((2, width), lambda i: (0, 0)),
+            pl.BlockSpec((width, cols), lambda i: (0, 0)),
+        ],
+        out_specs=[
+            pl.BlockSpec((block, 2 * width), lambda i: (i, 0)),
+            pl.BlockSpec((block, cols), lambda i: (i, 0)),
+        ],
+        out_shape=[
+            jax.ShapeDtypeStruct((slots, 2 * width), BF),
+            jax.ShapeDtypeStruct((slots, cols), BF),
+        ],
+        compiler_params=pltpu.CompilerParams(vmem_limit_bytes=VMEM_LIMIT),
+        cost_estimate=pl.CostEstimate(
+            flops=slots * width * cols * 4, transcendentals=0, bytes_accessed=slots * width * 8
+        ),
+        name="project",
+    )(x_all, scales, weight)
 
 
 def self_forward_kernel(n, block, info, qkv, mixed, logs, q_s, k_s, v_s):
@@ -164,7 +362,7 @@
     half = block // 2
     for c in range(n):
         for t in range(2):
-            place = lax.rem(me_c - c + n, n) * block + (me_t ^ t) * half
+            place = (me_c ^ c) * block + (me_t ^ t) * half
             place = pl.multiple_of(place, half)
             to = slice(c * block + t * half, c * block + t * half + half)
             rows = qkv[pl.ds(place, half), :]
@@ -211,7 +409,7 @@
         state = lax.fori_loop(0, whole, functools.partial(step, False), start)
         state = lax.fori_loop(whole, last, functools.partial(step, True), state)
         both = jnp.concatenate([acc / tot for _, tot, acc in state], axis=0)
-        place = pl.multiple_of(lax.rem(me_c - i + n, n) * block, block)
+        place = pl.multiple_of((me_c ^ i) * block, block)
         mixed[pl.ds(place, block), :] = both.T.astype(BF)
         for h in range(2):
             top, tot, _ = state[h]
@@ -228,7 +426,7 @@
     half = block // 2
     for c in range(n):
         for t in range(2):
-            place = lax.rem(me_c - c + n, n) * block + (me_t ^ t) * half
+            place = (me_c ^ c) * block + (me_t ^ t) * half
             place = pl.multiple_of(place, half)
             to = slice(c * block + t * half, c * block + t * half + half)
             rows = qkv[pl.ds(place, half), :]
@@ -239,7 +437,7 @@
                 k_s[h, to, :] = jnp.where(lanes_of(h, keys.shape), keys, jnp.zeros_like(keys))
                 v_s[h, to, :] = jnp.where(lanes_of(h, keys.shape), values, jnp.zeros_like(keys))
             kt_s[:, to] = keys.astype(F32).T.astype(BF)
-            at = pl.multiple_of(lax.rem(me_c - c + n, n) * block + t * half, half)
+            at = pl.multiple_of((me_c ^ c) * block + t * half, half)
             dout = grad[pl.ds(at, half), :]
             d_s[to, :] = dout
             both = (dout.astype(F32) * mixed[pl.ds(at, half), :].astype(F32)).T
@@ -285,7 +483,7 @@
         dk = jnp.where(first_head, state[0][0], state[1][0]).astype(BF)
         dv = jnp.where(first_head, state[0][1], state[1][1]).astype(BF)
         for t in range(2):
-            place = lax.rem(me_c - j + n, n) * block + (me_t ^ t) * half
+            place = (me_c ^ j) * block + (me_t ^ t) * half
             place = pl.multiple_of(place, half)
             grads[pl.ds(place, half), PAIR : 2 * PAIR] = dk[t * half : (t + 1) * half, :]
             grads[pl.ds(place, half), 2 * PAIR :] = dv[t * half : (t + 1) * half, :]
@@ -295,7 +493,7 @@
     for c in range(n):
         dq = (dq_s[:, c * block : (c + 1) * block] * HEAD_DIM**-0.5).T.astype(BF)
         for t in range(2):
-            place = lax.rem(me_c - c + n, n) * block + (me_t ^ t) * half
+            place = (me_c ^ c) * block + (me_t ^ t) * half
             place = pl.multiple_of(place, half)
             grads[pl.ds(place, half), :PAIR] = dq[t * half : (t + 1) * half, :]
 
@@ -421,7 +619,7 @@
         grid=(n,),
         in_specs=[
             pl.BlockSpec((rows, PAIR), lambda j, info: (0, j)),
-            pl.BlockSpec((1, keys, 2 * PAIR), lambda j, info: (lax.rem(info[1] - j + n, n), 0, 0)),
+            pl.BlockSpec((1, keys, 2 * PAIR), lambda j, info: (info[1] ^ j, 0, 0)),
         ],
         out_specs=[
             pl.BlockSpec((rows, PAIR), lambda j, info: (0, j)),
@@ -452,14 +650,14 @@
         grid=(n,),
         in_specs=[
             col,
-            pl.BlockSpec((1, keys, 2 * PAIR), lambda j, info: (lax.rem(info[1] - j + n, n), 0, 0)),
+            pl.BlockSpec((1, keys, 2 * PAIR), lambda j, info: (info[1] ^ j, 0, 0)),
             col,
             col,
             pl.BlockSpec((1, 2, rows), lambda j, info: (j, 0, 0)),
         ],
         out_specs=[
             col,
-            pl.BlockSpec((1, keys, 2 * PAIR), lambda j, info: (lax.rem(j - info[1] + n, n), 0, 0)),
+            pl.BlockSpec((1, keys, 2 * PAIR), lambda j, info: (info[1] ^ j, 0, 0)),
         ],
     )
     return pl.pallas_call(
@@ -509,7 +707,7 @@
     w_inner,
     w_outer,
 ):
-    n = lax.axis_size("ctx")
+    n, f = lax.axis_size("ctx"), lax.axis_size("fsdp")
     me_c, me_t = lax.axis_index("ctx"), lax.axis_index("tp")
     rows, width = inputs.shape[1], inputs.shape[2]
     half = rows // 2
@@ -519,63 +717,86 @@
     self_info = jnp.stack([seq_limit, me_c, me_t]).astype(jnp.int32)
     cross_info = jnp.stack([enc_limit, me_c, me_t]).astype(jnp.int32)
 
-    params = jnp.concatenate([norm_gains, norm_biases], axis=0)
-    params = jnp.concatenate(in_order(gather_direct(params, "ctx"), "ctx"), axis=1)
-    params = jnp.concatenate(in_order(gather_direct(params, "fsdp"), "fsdp"), axis=1)
-    params = params.astype(F32)
-    gains, biases = params[:4], params[4:]
+    enc_half = encoder_states.shape[1] // 2
+
+    def side(t):
+        return jnp.concatenate(
+            [
+                lax.dynamic_slice_in_dim(inputs[0], t * half, half, 0),
+                lax.dynamic_slice_in_dim(encoder_states[0], t * enc_half, enc_half, 0),
+            ],
+            axis=0,
+        )
 
     five = jnp.stack([w_query, w_key, w_value, w_cross_key, w_cross_value], axis=1)
     five = five.reshape(shard, 5, n, PAIR).transpose(2, 0, 1, 3).reshape(n, shard, 5 * PAIR)
-    five = jnp.concatenate(in_order(exchange_direct(five, "ctx"), "ctx"), axis=0)
-    five = jnp.concatenate(in_order(gather_direct(five, "fsdp"), "fsdp"), axis=0)
+    params = jnp.concatenate([norm_gains, norm_biases], axis=0).reshape(1, 1, 8 * shard)
+    params = jnp.pad(params, ((0, 0), (0, 15), (0, 5 * PAIR - 8 * shard)))
+    five = jnp.concatenate([five, jnp.broadcast_to(params, (n,) + params.shape[1:])], axis=1)
+    five = natural(exchange_direct(five, "ctx"), "ctx")
+    in_z = Gathering(w_inner, "ctx", False)
+    in_seen = [in_z.start()]
+    five = gather_direct(five, "fsdp")
+    while len(in_z.order) > 1:
+        in_seen.append(in_z.step())
+
+    seen_x = []
+    mine_rows = gather_offsets(tie(side(me_t), in_seen[0]), "ctx", False, seen_x, in_seen[-1])
+    w_in = Doubling(in_z.end())
+
+    w_three = jnp.concatenate([w_out.T, w_cross_query, w_cross_out.T], axis=1)
+    three_z = Gathering(w_three, "ctx", False)
+    three_z.start(seen_x[0])
+    outer_z = Gathering(w_outer.T, "ctx", False)
+    outer_z.start(seen_x[0])
+    while len(w_in.parts[0].order) > 1:
+        w_in.step(seen_x[0])
+    while len(three_z.order) > 1:
+        three_seen = three_z.step(seen_x[-1])
+        outer_z.step(three_seen)
+    w_three = Doubling(three_z.end())
+
+    came_rows = swap(jnp.concatenate(mine_rows[1:], axis=0))
+    size = half + enc_half
+    five = five.reshape(f * n, shard + 16, 5 * PAIR)
+    params = five[:, shard, : 8 * shard].reshape(f * n, 8, shard)
+    params = params.transpose(1, 0, 2).reshape(8, width).astype(F32)
+    gains, biases = params[:4], params[4:]
+    five = five[:, :shard].reshape(width, 5 * PAIR)
     w_qkv, w_ckv = five[:, : 3 * PAIR], five[:, 3 * PAIR :]
-
+    their_rows = [side(1 - me_t)] + [came_rows[k * size : (k + 1) * size] for k in range(n - 1)]
+    x_all = jnp.concatenate([v[:half] for k in range(n) for v in (mine_rows[k], their_rows[k])])
+    enc_found = [[v[half:] for v in (mine_rows[k], their_rows[k])] for k in range(n)]
+    enc_at = [[lax.select_n(me_t, e[0], e[1]), lax.select_n(me_t, e[1], e[0])] for e in enc_found]
+    enc_all = natural([jnp.concatenate(e, axis=0) for e in enc_at], "ctx")
+    ckv_own = nn(enc_all, w_ckv).astype(BF)
+    seen_ckv = []
+    ckv = jnp.stack(gather_offsets(ckv_own, "ctx", False, seen_ckv), axis=0)
+
+    scales = jnp.concatenate([gains[:1], biases[:1]], axis=0)
+    kept, qkv = project(tie(x_all, ckv_own, *w_in.came), scales, w_qkv)
+    outer_z.came = tie(outer_z.came, qkv)
+    w_outer_t = Doubling(outer_z.end())
+    three_first = w_three.came
+    while len(w_three.parts[0].order) > 1:
+        w_three.step(qkv)
+    mixed, logs = self_forward(self_info, tie(qkv, *three_first, seen_ckv[0]), n)
+    w_in = w_in.end(mixed)
+    w_three = w_three.end(mixed)
+    w_out_t, w_cq, w_co_t = w_three[:, :wide], w_three[:, wide : 2 * wide], w_three[:, 2 * wide :]
+    while len(w_outer_t.parts[0].order) > 1:
+        w_outer_t.step(mixed)
+    pieces = [mixed[:rows]] + [flip(mixed[k * rows : (k + 1) * rows], "ctx", k) for k in range(1, n)]
+    attn_flat = natural(pieces, "ctx", 1)
     hidden_x = inputs[0].astype(F32)
-    normed_a, scale_a = norm_parts(hidden_x)
-    attn_in = (normed_a * gains[0] + biases[0]).astype(BF)
-    own = lax.dynamic_slice_in_dim(attn_in, me_t * half, half, 0)
-    rest = lax.dynamic_slice_in_dim(attn_in, (1 - me_t) * half, half, 0)
-    came = gather_line(own, "ctx")[1:]
-    came_other = swap(jnp.concatenate(came, axis=0))
-    blocks = [own, rest]
-    for s in range(n - 1):
-        blocks += [came[s], came_other[s * half : (s + 1) * half]]
-    attn_all = jnp.concatenate(blocks, axis=0)
-
-    enc_half = encoder_states.shape[1] // 2
-    enc_own = lax.dynamic_slice_in_dim(encoder_states[0], me_t * enc_half, enc_half, 0)
-    enc_came = jnp.stack(in_order(gather_direct(enc_own, "ctx"), "ctx"), axis=0)
-    enc_came_other = swap(enc_came)
-    enc_all = jnp.stack(
-        [
-            jnp.where(me_t == 0, enc_came, enc_came_other),
-            jnp.where(me_t == 0, enc_came_other, enc_came),
-        ],
-        axis=1,
-    ).reshape(-1, width)
-
-    w_out_t = fetch_rows(w_out.T, False)
-    w_cq_co = fetch_rows(jnp.concatenate([w_cross_query, w_cross_out.T], axis=1), True)
-    w_cq, w_co_t = w_cq_co[:, :wide], w_cq_co[:, wide:]
-    w_in = fetch_rows(w_inner, True)
-    w_outer_t = fetch_rows(w_outer.T, False)
-
-    qkv = nn(attn_all, w_qkv).astype(BF)
-    mixed, logs = self_forward(self_info, qkv, n)
-    pieces = [mixed[:rows]] + [
-        shift(mixed[s * rows : (s + 1) * rows], "ctx", -s) for s in range(1, n)
-    ]
-    attn_flat = jnp.concatenate(in_order([pieces[(n - s) % n] for s in range(n)], "ctx"), axis=1)
     first = hidden_x + tp_total(nt(attn_flat, w_out_t))
 
-    ckv_own = nn(enc_all, w_ckv).astype(BF)
-    ckv = jnp.stack(gather_direct(ckv_own, "ctx"), axis=0)
     normed_c, scale_c = norm_parts(first)
     cross_in = (normed_c * gains[1] + biases[1]).astype(BF)
     cross_query = nn(cross_in, w_cq).astype(BF)
     cross_flat, cross_logs = cross_forward(cross_info, cross_query, ckv, n)
     second = first + tp_total(nt(cross_flat, w_co_t))
+    w_outer_t = w_outer_t.end(cross_flat)
 
     normed_f, scale_f = norm_parts(second)
     ffn_in = (normed_f * gains[2] + biases[2]).astype(BF)
@@ -592,63 +813,110 @@
     grad_y = cotangent[0].astype(F32) * valid
     grad_third, gain_y, bias_y = norm_back(grad_y, normed_y, scale_y, gains[3])
     g3 = grad_third.astype(BF)
+    outer = Halving([(g3, active)])
     grad_active = gate_pullback(nn(g3, w_outer_t))[0].astype(BF)
-    grad_outer = return_rows(tn(g3, active).astype(BF), True).T
-    grad_inner = return_rows(tn(ffn_in, grad_active).astype(BF), False)
-    grad_ffn_in = tp_total(nt(grad_active, w_in))
+    partial = nt(grad_active, w_in).astype(BF)
+    inside = Halving([(tie(ffn_in, partial), grad_active)], *outer.flight())
+    grad_ffn_in = partial.astype(F32) + swap(partial).astype(F32)
     part_f, gain_f, bias_f = norm_back(grad_ffn_in, normed_f, scale_f, gains[2])
     grad_second = grad_third + part_f
     g2 = grad_second.astype(BF)
 
     grad_cross = nn(g2, w_co_t).astype(BF)
     grad_cq, dkv = cross_backward(
-        cross_info, cross_query, ckv, cross_flat, grad_cross, cross_logs, n
-    )
-    grad_ckv = total([dkv[0]] + [shift(dkv[s], "ctx", s) for s in range(1, n)]).astype(BF)
-    pair = jnp.concatenate(
-        [tn(cross_in, grad_cq).astype(BF), tn(g2, cross_flat).astype(BF)], axis=1
-    )
-    pair = return_rows(pair, True)
-    grad_w_cq, grad_w_co = pair[:, :wide], pair[:, wide:].T
-    grad_cross_in = tp_total(nt(grad_cq, w_cq))
+        cross_info,
+        cross_query,
+        ckv,
+        cross_flat,
+        tie(grad_cross, *outer.held(), *inside.held()),
+        cross_logs,
+        n,
+    )
+    partial = nt(grad_cq, w_cq).astype(BF)
+    outer.step(partial)
+    grad_cross_in = partial.astype(F32) + swap(partial).astype(F32)
+    grad_cross_in = tie(grad_cross_in, *outer.held())
     part_c, gain_c, bias_c = norm_back(grad_cross_in, normed_c, scale_c, gains[1])
     grad_first = grad_second + part_c
     g1 = grad_first.astype(BF)
 
-    enc_part = tp_total(nt(grad_ckv, w_ckv)).astype(BF).reshape(n, 2, enc_half, width)
-    enc_part = lax.dynamic_index_in_dim(enc_part, me_t, 1, keepdims=False)
-    grad_encoder = tp_join(total(exchange_direct(enc_part, "ctx")))
-
-    grad_w_out = return_rows(tn(g1, attn_flat).astype(BF), False).T
     grad_attn = nn(g1, w_out_t).astype(BF)
     grad_attn = grad_attn.reshape(rows, n, PAIR).transpose(1, 0, 2)
-    dmixed = jnp.concatenate(exchange_direct(grad_attn, "ctx"), axis=0)
+    dmixed = exchange_direct(grad_attn, "ctx")
+    outer.step(dmixed[0])
+    three = Halving(
+        [(tie(g1, dmixed[0]), attn_flat), (cross_in, grad_cq), (g2, cross_flat)], *inside.flight()
+    )
+    inside.step(dmixed[0])
+
+    grad_ckv = scatter_offsets([tie(dkv, dmixed[0])[k] for k in range(n)], "ctx").astype(BF)
+
+    dmixed = tie(
+        jnp.concatenate(dmixed, axis=0), *outer.held(), *inside.held(), *three.held(), grad_ckv
+    )
     dqkv = self_backward(self_info, qkv, mixed, dmixed, logs, n)
-    part = nt(dqkv, w_qkv).astype(BF).reshape(n, 2, half, width)
-    part = (part[:, 0].astype(F32) + swap(part[:, 1]).astype(F32)).astype(BF)
-    grad_attn_in = total([part[0]] + [shift(part[s], "ctx", -s) for s in range(1, n)])
-
-    dfive = jnp.concatenate([tn(attn_all, dqkv), tn(enc_all, grad_ckv)], axis=1).astype(BF)
-    f = lax.axis_size("fsdp")
-    dfive = total(exchange_direct(dfive.reshape(f, n * shard, 5 * PAIR), "fsdp")).astype(BF)
-    dfive = in_order(exchange_direct(dfive.reshape(n, shard, 5 * PAIR), "ctx"), "ctx")
-    dfive = jnp.stack(dfive, axis=0).reshape(n, shard, 5, PAIR).transpose(2, 1, 0, 3)
+
+    part = nt(tie(dqkv, *three.flight(), *inside.flight(), *outer.flight()), w_qkv).astype(BF)
+    away = jnp.concatenate([part[(2 * k + 1) * half : (2 * k + 2) * half] for k in range(n)])
+    came_part = swap(away)
+    inside.step(away)
+    for leg in outer.parts:
+        leg.came = tie(leg.came, away)
+        while leg.legs:
+            leg.step()
+    three.step(away)
+    came_part = tie(came_part, *outer.held(), *inside.held(), *three.held())
+    part = [
+        (
+            part[2 * k * half : (2 * k + 1) * half].astype(F32)
+            + came_part[k * half : (k + 1) * half].astype(F32)
+        ).astype(BF)
+        for k in range(n)
+    ]
+    dqkv_late = tie(dqkv, *part)
+    seen_part = []
+    grad_attn_in = scatter_offsets(part, "ctx", seen_part)
+
+    both = tn(kept, dqkv_late)
+    gain_a = jnp.sum(both[width:] * w_qkv.astype(F32), axis=1)
+    bias_a = nt(jnp.sum(dqkv_late.astype(F32), axis=0, keepdims=True), w_qkv.astype(F32))[0]
+    norm_grads = jnp.stack(
+        [gain_a, 0.5 * gain_c, 0.5 * gain_f, 0.5 * gain_y]
+        + [bias_a, 0.5 * bias_c, 0.5 * bias_f, 0.5 * bias_y]
+    )
+    norm_grads = norm_grads + swap(norm_grads)
+    norm_grads = norm_grads.reshape(8, f * n, shard).transpose(1, 0, 2).reshape(f * n, 1, 8 * shard)
+    norm_grads = jnp.pad(norm_grads, ((0, 0), (0, 15), (0, 5 * PAIR - 8 * shard)))
+    dfive = jnp.concatenate([both[:width], tn(enc_all, grad_ckv)], axis=1)
+    dfive = jnp.concatenate([dfive.reshape(f * n, shard, 5 * PAIR), norm_grads], axis=1).astype(BF)
+    dfive = scatter_value(dfive.reshape(f * n * (shard + 16), 5 * PAIR), [("fsdp", True)])
+    while dfive.legs:
+        dfive.step()
+    dfive = dfive.end().astype(BF).reshape(n, shard + 16, 5 * PAIR)
+    dfive = natural([v[None] for v in exchange_direct(dfive, "ctx")], "ctx")
+    norm_grads = jnp.sum(dfive[:, shard, : 8 * shard].astype(F32), axis=0).reshape(8, shard)
+    dfive = dfive[:, :shard].reshape(n, shard, 5, PAIR).transpose(2, 1, 0, 3)
     dfive = dfive.reshape(5, shard, wide).astype(F32)
+
+    three.step(both)
+    for leg in inside.parts + three.parts:
+        leg.came = tie(leg.came, seen_part[0])
+        while leg.legs:
+            leg.step()
+    three = three.end()
+    grad_outer, grad_inner = outer.end(seen_part[0]).T, inside.end()
+    enc_part = tp_total(nt(tie(grad_ckv, *part), w_ckv)).astype(BF)
+    enc = scatter_value(enc_part, [("ctx", True)])
+    while len(enc.legs) > 0:
+        enc.step()
+    grad_encoder = enc.end()
 
     def mine(values):
         return lax.dynamic_slice_in_dim(values, me_t * half, half, 0)
 
-    part_a, gain_a, bias_a = norm_back(grad_attn_in, mine(normed_a), mine(scale_a), gains[0])
+    normed_a, scale_a = norm_parts(mine(hidden_x))
+    part_a, _, _ = norm_back(grad_attn_in, normed_a, scale_a, gains[0])
     grad_inputs = tp_join(mine(grad_first) + part_a)
-    pair_a = jnp.stack([gain_a, bias_a])
-    pair_a = pair_a + swap(pair_a)
-    norm_grads = jnp.stack(
-        [pair_a[0], gain_c, gain_f, gain_y, pair_a[1], bias_c, bias_f, bias_y]
-    )
-    norm_grads = norm_grads.reshape(8, f, n * shard).transpose(1, 0, 2)
-    norm_grads = total(exchange_direct(norm_grads, "fsdp"))
-    norm_grads = norm_grads.reshape(8, n, shard).transpose(1, 0, 2)
-    norm_grads = total(exchange_direct(norm_grads, "ctx"))
 
     return (
         output[None],
@@ -659,11 +927,11 @@
         dfive[0],
         dfive[1],
         dfive[2],
-        grad_w_out,
-        grad_w_cq,
+        three[:, :wide].T,
+        three[:, wide : 2 * wide],
         dfive[3],
         dfive[4],
-        grad_w_co,
+        three[:, 2 * wide :].T,
         grad_inner,
         grad_outer,
     )

time: 581 us -> 548 us (0.943)
  starting transfers between devices: 176 us -> 82.4 us
  local copies, waits for them, and re-layouts: 44.9 us -> 65.9 us
  Pallas kernels: 34.4 us -> 50 us
  other arithmetic: 70.4 us -> 85.7 us
    ppermute x115 -> x73, starting transfers between devices: 176 us -> 82.4 us  [flip(): return lax.ppermute(value, axis, [(i, i ^ mask) for i in range(n)])]
    unnamed x171 -> x217, local copies, waits for them, and re-layouts: 16.3 us -> 31.1 us
    convert_element_type x13 -> x30, other arithmetic: 15.7 us -> 27.8 us  [the longest x11 11.7 us: part(): (held + half_rows(self.came, index, bit, self.bits).astype(F32)).astype(BF)]
    slice x2 -> x21, local copies, waits for them, and re-layouts: 0.04 us -> 11.5 us  [the longest x3 2.93 us: __init__(): away[place * cut:(place + 1) * cut]]
    pallas_call x0 -> x1, Pallas kernels: none -> 9.03 us  [project(): pl.pallas_call(project_kernel, grid=(slots // block,), in_specs=[pl.Block...]
    concatenate x16 -> x38, other arithmetic: 7.83 us -> 14.9 us  [the longest x9 3.34 us: start(): sent = sent[0] if len(sent) == 1 else jnp.concatenate(sent, axis=0)]
    dynamic_slice x9 -> x7, local copies, waits for them, and re-layouts: 10.4 us -> 3.41 us  [the longest x5 2.52 us: half_rows(): lax.dynamic_slice_in_dim(view, index, 1, 1).reshape(rows, held.shape[1])]
    add x8 -> x3, other arithmetic: 8.51 us -> 2.26 us  [the longest x2 1.88 us: end(): return self.held.astype(F32) + self.came.astype(F32)]
  transfers between devices with their start and end apart: 115 -> 73, of which waited for: 36 -> 33; matrix products, arithmetic and copies ran while one was open for 21% -> 26% of each run, Pallas kernels for 6% -> 9%
where the time goes in v2:
time: 548 us; the launch traced here: 537 us
  waiting for transfers between devices  204 us (37%)
  other arithmetic  85.7 us (16%)
  starting transfers between devices  82.4 us (15%)
  local copies, waits for them, and re-layouts  65.9 us (12%)
  Pallas kernels  50 us (9%)
  matrix products  44.6 us (8%)
    ppermute x73, waiting for transfers between devices, flip(): return lax.ppermute(value, axis, [(i, i ^ mask) for i in range(n)])  204 us
    ppermute x73, starting transfers between devices, flip(): return lax.ppermute(value, axis, [(i, i ^ mask) for i in range(n)])  82.4 us
    unnamed x217, local copies, waits for them, and re-layouts  31.1 us
    pallas_call x1, Pallas kernels, self_backward(): pl.pallas_call(functools.partial(self_backward_kernel, n, block), out_sha...  18.2 us
    dot_general x12, matrix products, tn(): lax.dot_general(left, right, (((0,), (0,)), ((), ())), preferred_element_...  17.3 us
    dot_general x8, matrix products, nt(): lax.dot_general(left, right, (((1,), (1,)), ((), ())), preferred_element_...  14.5 us
    pallas_call x1, Pallas kernels, self_forward(): pl.pallas_call(functools.partial(self_forward_kernel, n, block), out_shap...  13.3 us
    dot_general x6, matrix products, nn(): return jnp.dot(left, right, preferred_element_type=F32)  12.8 us
  transfers between devices with their start and end apart: 73, of which 33 were waited for; matrix products, arithmetic and copies ran while one was open for 26% of the time, Pallas kernels for 9%

profile of v2, /device:TPU:0, one launch (start us, length us, event | category | flops | bytes accessed | tf_op | source)
XLA Modules:
  0.0 537.0 jit_solution(2136924634712143275)
XLA Ops:
  8.6 3.0 collective-permute-start.5
  23.6 4.9 collective-permute-done.6
  49.9 14.6 %collective-permute-done.2 = bf16[128,2048]{1,0:T(8,128)(2,1)} collective-permute-done((bf16[128,2048]{1,0:T(8,128)(2,1)}, bf16[128,2048]{1,0:T(8,128)(2,1)}, u32[]{:S(2)}, u32[]{:S(2)}) %collective-permute-start.2) | collective-permute-done | bytes 524320 | tf_op jit(solution)/shard_map/ppermute | solution.py:55
  72.2 4.1 collective-permute-done.15
  76.5 22.4 %collective-permute-done.28 = bf16[64,2048]{1,0:T(8,128)(2,1)S(1)} collective-permute-done((bf16[64,2048]{1,0:T(8,128)(2,1)S(1)}, bf16[64,2048]{1,0:T(8,128)(2,1)S(1)}, u32[]{:S(2)}, u32[]{:S(2)}) %collective-permute-start.28) | collective-permute-done | bytes 262176 | tf_op jit(solution)/shard_map/ppermute | solution.py:55
  106.6 7.4 %collective-permute-done.16 = bf16[128,1536]{1,0:T(8,128)(2,1)S(1)} collective-permute-done((bf16[128,1536]{1,0:T(8,128)(2,1)S(1)}, bf16[128,1536]{1,0:T(8,128)(2,1)S(1)}, u32[]{:S(2)}, u32[]{:S(2)}) %collective-permute-start.16) | collective-permute-done | bytes 393248 | tf_op jit(solution)/shard_map/ppermute | solution.py:55
  126.7 3.5 collective-permute-done.14
  130.2 9.0 %project.1 = (bf16[2048,2048]{1,0:T(8,128)(2,1)}, bf16[2048,384]{1,0:T(8,128)(2,1)S(1)}) custom-call(bf16[2048,1024]{1,0:T(8,128)(2,1)} %slice_dynamic-update-slice_fusion.x_ref, f32[2,1024]{1,0:T(2,128)S(1)} %pad_maximum_fusion.64.scales, bf16[1024,384]{1,0:T(8,128)(2,1)S(1)} %slice.708.weight), custom_call_target="tpu_custom_call" | custom-call | flops 3221225472 | bytes 16777216 | tf_op jit(solution)/shard_map/project/pallas_call | solution.py:336
  143.5 13.3 %self_forward.1 = (bf16[2048,128]{1,0:T(8,128)(2,1)S(1)}, f32[2,2048]{1,0:T(2,128)S(1)}) custom-call(s32[3]{0:T(128)S(1)} %add_add_fusion.2.info, bf16[2048,384]{1,0:T(8,128)(2,1)S(1)} %get-tuple-element.80.qkv), custom_call_target="tpu_custom_call" | custom-call | flops 2147483648 | bytes 2097152 | tf_op jit(solution)/shard_map/self_forward/pallas_call | solution.py:567
  165.6 4.2 collective-permute-done.21
  173.4 22.1 %collective-permute-done.30 = bf16[128,2048]{1,0:T(8,128)(2,1)S(1)} collective-permute-done((bf16[128,2048]{1,0:T(8,128)(2,1)S(1)}, bf16[128,2048]{1,0:T(8,128)(2,1)S(1)}, u32[]{:S(2)}, u32[]{:S(2)}) %collective-permute-start.30) | collective-permute-done | bytes 524320 | tf_op jit(solution)/shard_map/ppermute | solution.py:55
  204.1 4.3 cross_forward.1
  208.4 5.5 %collective-permute-done.33 = bf16[256,2048]{1,0:T(8,128)(2,1)S(1)} collective-permute-done((bf16[256,2048]{1,0:T(8,128)(2,1)S(1)}, bf16[256,2048]{1,0:T(8,128)(2,1)S(1)}, u32[]{:S(2)}, u32[]{:S(2)}) %collective-permute-start.33) | collective-permute-done | bytes 1048608 | tf_op jit(solution)/shard_map/ppermute | solution.py:55
  225.1 3.7 convolution_convert_fusion.9
  240.3 5.6 %fusion.3 = bf16[512,2048]{1,0:T(8,128)(2,1)S(1)} fusion(f32[512,2048]{1,0:T(8,128)S(1)} %copy-done.97, bf16[512,1024]{1,0:T(8,128)(2,1)S(1)} %fusion.90, bf16[1024,2048]{1,0:T(8,128)(2,1)S(1)} %copy-done.77), kind=kOutput, calls=%fused_computation.7 | convolution fusion | flops 2172649472 | bytes 11534336 | tf_op jit(solution)/shard_map/dot_general | solution.py:21
  262.8 2.9 fusion.92
  267.7 5.1 cross_backward.1
  302.1 3.4 collective-permute-done.44
  338.8 3.8 collective-permute-start.47
  343.7 2.9 collective-permute-done.47
  350.7 18.2 %self_backward.1 = bf16[2048,384]{1,0:T(8,128)(2,1)S(1)} custom-call(s32[3]{0:T(128)S(1)} %add_add_fusion.2.info, bf16[2048,384]{1,0:T(8,128)(2,1)S(1)} %copy-done.1, bf16[2048,128]{1,0:T(8,128)(2,1)S(1)} %get-tuple-element.81.mixed, bf16[2048,128]{1,0:T(8,128)(2,1)S(1)} %pad_maximum_fusion.27.grad, f32[2,2048]{1,0:T(2,128)S(1)} %get-tuple-element.112.logs), custom_call_target="tpu_custom_call" | custom-call | flops 5368709120 | bytes 5242880 | tf_op jit(solution)/shard_map/self_backward/pallas_call | solution.py:592
  386.5 30.9 %collective-permute-done.72 = bf16[64,2048]{1,0:T(8,128)(2,1)S(1)} collective-permute-done((bf16[64,2048]{1,0:T(8,128)(2,1)S(1)}, bf16[64,2048]{1,0:T(8,128)(2,1)S(1)}, u32[]{:S(2)}, u32[]{:S(2)}) %collective-permute-start.72) | collective-permute-done | bytes 262176 | tf_op jit(solution)/shard_map/ppermute | solution.py:55
  423.8 21.8 %collective-permute-done.71 = bf16[64,2048]{1,0:T(8,128)(2,1)S(1)} collective-permute-done((bf16[64,2048]{1,0:T(8,128)(2,1)S(1)}, bf16[64,2048]{1,0:T(8,128)(2,1)S(1)}, u32[]{:S(2)}, u32[]{:S(2)}) %collective-permute-start.71) | collective-permute-done | bytes 262176 | tf_op jit(solution)/shard_map/ppermute | solution.py:55
  446.5 9.3 %collective-permute-done.55 = bf16[256,1024]{1,0:T(8,128)(2,1)S(1)} collective-permute-done((bf16[256,1024]{1,0:T(8,128)(2,1)S(1)}, bf16[256,1024]{1,0:T(8,128)(2,1)S(1)}, u32[]{:S(2)}, u32[]{:S(2)}) %collective-permute-start.55) | collective-permute-done | bytes 524320 | tf_op jit(solution)/shard_map/ppermute | solution.py:55
  457.7 3.6 fusion.114
  473.0 3.1 copy.79
  482.2 3.3 multiply_add_fusion.4
  489.3 2.8 collective-permute-start.69
  493.8 8.0 %collective-permute-done.69 = bf16[64,1536]{1,0:T(8,128)(2,1)S(1)} collective-permute-done((bf16[64,1536]{1,0:T(8,128)(2,1)S(1)}, bf16[64,1536]{1,0:T(8,128)(2,1)S(1)}, u32[]{:S(2)}, u32[]{:S(2)}) %collective-permute-start.69) | collective-permute-done | bytes 196640 | tf_op jit(solution)/shard_map/ppermute | solution.py:55
  507.4 5.4 %collective-permute-done.59 = bf16[64,1024]{1,0:T(8,128)(2,1)S(1)} collective-permute-done((bf16[64,1024]{1,0:T(8,128)(2,1)S(1)}, bf16[64,1024]{1,0:T(8,128)(2,1)S(1)}, u32[]{:S(2)}, u32[]{:S(2)}) %collective-permute-start.59) | collective-permute-done | bytes 131104 | tf_op jit(solution)/shard_map/ppermute | solution.py:55
  515.1 3.6 collective-permute-done.62
  524.9 6.0 %collective-permute-done.64 = bf16[80,640]{1,0:T(8,128)(2,1)S(1)} collective-permute-done((bf16[80,640]{1,0:T(8,128)(2,1)S(1)}, bf16[80,640]{1,0:T(8,128)(2,1)S(1)}, u32[]{:S(2)}, u32[]{:S(2)}) %collective-permute-start.64) | collective-permute-done | bytes 102432 | tf_op jit(solution)/shard_map/ppermute | solution.py:55
  (608 shorter events, 271.1 us)
Async XLA Ops:
  35.0 32.4 %collective-permute-start.1 = (bf16[288,1024]{1,0:T(8,128)(2,1)S(1)}, bf16[288,1024]{1,0:T(8,128)(2,1)S(1)}, u32[]{:S(2)}, u32[]{:S(2)}) collective-permute-start(bf16[288,1024]{1,0:T(8,128)(2,1)S(1)} %copy-done.15), channel_id=1, source_target_pairs={{0,4},{2,6},{4,0},{6,2},{1,5},{3,7},{5,1},{7,3},{8,12},{10,14},{12... | collective-permute-start | bytes 1769480 | tf_op jit(solution)/shard_map/ppermute | solution.py:55
  65.9 33.1 %collective-permute-start.11 = (bf16[128,2048]{1,0:T(8,128)(2,1)S(1)}, bf16[128,2048]{1,0:T(8,128)(2,1)S(1)}, u32[]{:S(2)}, u32[]{:S(2)}) collective-permute-start(bf16[128,2048]{1,0:T(8,128)(2,1)S(1)} %pad_maximum_fusion.20), channel_id=1, source_target_pairs={{0,8},{8,0},{16,24},{24,16},{1,9},{9,1},{17,25},{25,17},{2,10},{10... | collective-permute-start | bytes 1572872 | tf_op jit(solution)/shard_map/ppermute | solution.py:55
  67.5 33.0 %collective-permute-start.13 = (bf16[128,2048]{1,0:T(8,128)(2,1)S(1)}, bf16[128,2048]{1,0:T(8,128)(2,1)S(1)}, u32[]{:S(2)}, u32[]{:S(2)}) collective-permute-start(bf16[128,2048]{1,0:T(8,128)(2,1)S(1)} %pad_maximum_fusion.21), channel_id=1, source_target_pairs={{0,16},{8,24},{16,0},{24,8},{1,17},{9,25},{17,1},{25,9},{2,18},{10... | collective-permute-start | bytes 1572872 | tf_op jit(solution)/shard_map/ppermute | solution.py:55
  69.1 32.7 %collective-permute-start.3 = (bf16[576,1024]{1,0:T(8,128)(2,1)S(1)}, bf16[576,1024]{1,0:T(8,128)(2,1)S(1)}, u32[]{:S(2)}, u32[]{:S(2)}) collective-permute-start(bf16[576,1024]{1,0:T(8,128)(2,1)S(1)} %pad_maximum_fusion.6), channel_id=1, source_target_pairs={{0,2},{2,0},{4,6},{6,4},{1,3},{3,1},{5,7},{7,5},{8,10},{10,8},{12,... | collective-permute-start | bytes 3538952 | tf_op jit(solution)/shard_map/ppermute | solution.py:55
  71.2 27.6 %collective-permute-start.28 = (bf16[64,2048]{1,0:T(8,128)(2,1)S(1)}, bf16[64,2048]{1,0:T(8,128)(2,1)S(1)}, u32[]{:S(2)}, u32[]{:S(2)}) collective-permute-start(bf16[64,2048]{1,0:T(8,128)(2,1)S(1)} %bitcast.244), channel_id=1, source_target_pairs={{0,4},{2,6},{4,0},{6,2},{1,5},{3,7},{5,1},{7,3},{8,12},{10,14},{12... | collective-permute-start | bytes 786440 | tf_op jit(solution)/shard_map/ppermute | solution.py:55
  99.3 25.1 %collective-permute-start.12 = (bf16[256,2048]{1,0:T(8,128)(2,1)S(1)}, bf16[256,2048]{1,0:T(8,128)(2,1)S(1)}, u32[]{:S(2)}, u32[]{:S(2)}) collective-permute-start(bf16[256,2048]{1,0:T(8,128)(2,1)S(1)} %pad_maximum_fusion.7), channel_id=1, source_target_pairs={{0,16},{8,24},{16,0},{24,8},{1,17},{9,25},{17,1},{25,9},{2,18},{10... | collective-permute-start | bytes 3145736 | tf_op jit(solution)/shard_map/ppermute | solution.py:55
  104.2 26.1 %collective-permute-start.14 = (bf16[256,2048]{1,0:T(8,128)(2,1)S(1)}, bf16[256,2048]{1,0:T(8,128)(2,1)S(1)}, u32[]{:S(2)}, u32[]{:S(2)}) collective-permute-start(bf16[256,2048]{1,0:T(8,128)(2,1)S(1)} %pad_maximum_fusion.8), channel_id=1, source_target_pairs={{0,8},{8,0},{16,24},{24,16},{1,9},{9,1},{17,25},{25,17},{2,10},{10... | collective-permute-start | bytes 3145736 | tf_op jit(solution)/shard_map/ppermute | solution.py:55
  114.1 26.9 %collective-permute-start.18 = (bf16[128,1536]{1,0:T(8,128)(2,1)S(1)}, bf16[128,1536]{1,0:T(8,128)(2,1)}, u32[]{:S(2)}, u32[]{:S(2)}) collective-permute-start(bf16[128,1536]{1,0:T(8,128)(2,1)S(1)} %pad_maximum_fusion.31), channel_id=1, source_target_pairs={{0,16},{8,24},{16,0},{24,8},{1,17},{9,25},{17,1},{25,9},{2,18},{10... | collective-permute-start | bytes 1179656 | tf_op jit(solution)/shard_map/ppermute | solution.py:55
  139.4 33.3 %collective-permute-start.32 = (bf16[128,2048]{1,0:T(8,128)(2,1)S(1)}, bf16[128,2048]{1,0:T(8,128)(2,1)S(1)}, u32[]{:S(2)}, u32[]{:S(2)}) collective-permute-start(bf16[128,2048]{1,0:T(8,128)(2,1)S(1)} %pad_maximum_fusion.26), channel_id=1, source_target_pairs={{0,16},{8,24},{16,0},{24,8},{1,17},{9,25},{17,1},{25,9},{2,18},{10... | collective-permute-start | bytes 1572872 | tf_op jit(solution)/shard_map/ppermute | solution.py:55
  143.4 29.2 %collective-permute-start.26 = (bf16[512,256]{1,0:T(8,128)(2,1)S(1)}, bf16[512,256]{1,0:T(8,128)(2,1)S(1)}, u32[]{:S(2)}, u32[]{:S(2)}) collective-permute-start(bf16[512,256]{1,0:T(8,128)(2,1)S(1)} %pad_maximum_fusion.35), channel_id=1, source_target_pairs={{0,2},{2,0},{4,6},{6,4},{1,3},{3,1},{5,7},{7,5},{8,10},{10,8},{12,... | collective-permute-start | bytes 786440 | tf_op jit(solution)/shard_map/ppermute | solution.py:55
  162.9 34.5 %collective-permute-start.24 = (bf16[256,1536]{1,0:T(8,128)(2,1)}, bf16[256,1536]{1,0:T(8,128)(2,1)S(1)}, u32[]{:S(2)}, u32[]{:S(2)}) collective-permute-start(bf16[256,1536]{1,0:T(8,128)(2,1)} %pad_maximum_fusion.15), channel_id=1, source_target_pairs={{0,8},{8,0},{16,24},{24,16},{1,9},{9,1},{17,25},{25,17},{2,10},{10... | collective-permute-start | bytes 2359304 | tf_op jit(solution)/shard_map/ppermute | solution.py:55
  169.7 27.6 %collective-permute-start.23 = (bf16[256,1536]{1,0:T(8,128)(2,1)S(1)}, bf16[256,1536]{1,0:T(8,128)(2,1)S(1)}, u32[]{:S(2)}, u32[]{:S(2)}) collective-permute-start(bf16[256,1536]{1,0:T(8,128)(2,1)S(1)} %pad_maximum_fusion.14), channel_id=1, source_target_pairs={{0,16},{8,24},{16,0},{24,8},{1,17},{9,25},{17,1},{25,9},{2,18},{10... | collective-permute-start | bytes 2359304 | tf_op jit(solution)/shard_map/ppermute | solution.py:55
  169.8 25.7 %collective-permute-start.30 = (bf16[128,2048]{1,0:T(8,128)(2,1)S(1)}, bf16[128,2048]{1,0:T(8,128)(2,1)S(1)}, u32[]{:S(2)}, u32[]{:S(2)}) collective-permute-start(bf16[128,2048]{1,0:T(8,128)(2,1)S(1)} %pad_maximum_fusion.25), channel_id=1, source_target_pairs={{0,8},{8,0},{16,24},{24,16},{1,9},{9,1},{17,25},{25,17},{2,10},{10... | collective-permute-start | bytes 1572872 | tf_op jit(solution)/shard_map/ppermute | solution.py:55
  173.3 40.6 %collective-permute-start.33 = (bf16[256,2048]{1,0:T(8,128)(2,1)S(1)}, bf16[256,2048]{1,0:T(8,128)(2,1)S(1)}, u32[]{:S(2)}, u32[]{:S(2)}) collective-permute-start(bf16[256,2048]{1,0:T(8,128)(2,1)S(1)} %pad_maximum_fusion.10), channel_id=1, source_target_pairs={{0,8},{8,0},{16,24},{24,16},{1,9},{9,1},{17,25},{25,17},{2,10},{10... | collective-permute-start | bytes 3145736 | tf_op jit(solution)/shard_map/ppermute | solution.py:55
  251.0 25.3 %collective-permute-start.38 = (bf16[256,2048]{1,0:T(8,128)(2,1)S(1)}, bf16[256,2048]{1,0:T(8,128)(2,1)S(1)}, u32[]{:S(2)}, u32[]{:S(2)}) collective-permute-start(bf16[256,2048]{1,0:T(8,128)(2,1)S(1)} %get-tuple-element.181), channel_id=1, source_target_pairs={{0,16},{8,24},{16,0},{24,8},{1,17},{9,25},{17,1},{25,9},{2,18},{10... | collective-permute-start | bytes 3145736 | tf_op jit(solution)/shard_map/ppermute | solution.py:55
  252.3 25.3 %collective-permute-start.37 = (bf16[256,2048]{1,0:T(8,128)(2,1)S(1)}, bf16[256,2048]{1,0:T(8,128)(2,1)S(1)}, u32[]{:S(2)}, u32[]{:S(2)}) collective-permute-start(bf16[256,2048]{1,0:T(8,128)(2,1)S(1)} %get-tuple-element.182), channel_id=1, source_target_pairs={{0,8},{8,0},{16,24},{24,16},{1,9},{9,1},{17,25},{25,17},{2,10},{10... | collective-permute-start | bytes 3145736 | tf_op jit(solution)/shard_map/ppermute | solution.py:55
  279.1 26.4 %collective-permute-start.44 = (bf16[256,2048]{1,0:T(8,128)(2,1)}, bf16[256,2048]{1,0:T(8,128)(2,1)}, u32[]{:S(2)}, u32[]{:S(2)}) collective-permute-start(bf16[256,2048]{1,0:T(8,128)(2,1)} %get-tuple-element.176), channel_id=1, source_target_pairs={{0,8},{8,0},{16,24},{24,16},{1,9},{9,1},{17,25},{25,17},{2,10},{10... | collective-permute-start | bytes 3145736 | tf_op jit(solution)/shard_map/ppermute | solution.py:55
  280.8 26.4 %collective-permute-start.45 = (bf16[256,2048]{1,0:T(8,128)(2,1)}, bf16[256,2048]{1,0:T(8,128)(2,1)}, u32[]{:S(2)}, u32[]{:S(2)}) collective-permute-start(bf16[256,2048]{1,0:T(8,128)(2,1)} %get-tuple-element.175), channel_id=1, source_target_pairs={{0,16},{8,24},{16,0},{24,8},{1,17},{9,25},{17,1},{25,9},{2,18},{10... | collective-permute-start | bytes 3145736 | tf_op jit(solution)/shard_map/ppermute | solution.py:55
  282.8 35.7 %collective-permute-start.42 = (bf16[128,2048]{1,0:T(8,128)(2,1)}, bf16[128,2048]{1,0:T(8,128)(2,1)}, u32[]{:S(2)}, u32[]{:S(2)}) collective-permute-start(bf16[128,2048]{1,0:T(8,128)(2,1)} %get-tuple-element.177), channel_id=1, source_target_pairs={{0,16},{8,24},{16,0},{24,8},{1,17},{9,25},{17,1},{25,9},{2,18},{10... | collective-permute-start | bytes 1572872 | tf_op jit(solution)/shard_map/ppermute | solution.py:55
  285.3 37.5 %collective-permute-start.43 = (bf16[128,2048]{1,0:T(8,128)(2,1)}, bf16[128,2048]{1,0:T(8,128)(2,1)}, u32[]{:S(2)}, u32[]{:S(2)}) collective-permute-start(bf16[128,2048]{1,0:T(8,128)(2,1)} %get-tuple-element.179), channel_id=1, source_target_pairs={{0,8},{8,0},{16,24},{24,16},{1,9},{9,1},{17,25},{25,17},{2,10},{10... | collective-permute-start | bytes 1572872 | tf_op jit(solution)/shard_map/ppermute | solution.py:55
  308.5 60.5 %collective-permute-start.48 = (bf16[256,1536]{0,1:T(8,128)(2,1)}, bf16[256,1536]{0,1:T(8,128)(2,1)}, u32[]{:S(2)}, u32[]{:S(2)}) collective-permute-start(bf16[256,1536]{0,1:T(8,128)(2,1)} %get-tuple-element.199), channel_id=1, source_target_pairs={{0,8},{8,0},{16,24},{24,16},{1,9},{9,1},{17,25},{25,17},{2,10},{10... | collective-permute-start | bytes 2359304 | tf_op jit(solution)/shard_map/ppermute | solution.py:55
  308.8 61.2 %collective-permute-start.49 = (bf16[256,1536]{0,1:T(8,128)(2,1)}, bf16[256,1536]{0,1:T(8,128)(2,1)}, u32[]{:S(2)}, u32[]{:S(2)}) collective-permute-start(bf16[256,1536]{0,1:T(8,128)(2,1)} %get-tuple-element.198), channel_id=1, source_target_pairs={{0,16},{8,24},{16,0},{24,8},{1,17},{9,25},{17,1},{25,9},{2,18},{10... | collective-permute-start | bytes 2359304 | tf_op jit(solution)/shard_map/ppermute | solution.py:55
  335.5 33.4 %collective-permute-start.51 = (bf16[128,2048]{1,0:T(8,128)(2,1)}, bf16[128,2048]{1,0:T(8,128)(2,1)S(1)}, u32[]{:S(2)}, u32[]{:S(2)}) collective-permute-start(bf16[128,2048]{1,0:T(8,128)(2,1)} %get-tuple-element.171), channel_id=1, source_target_pairs={{0,8},{8,0},{16,24},{24,16},{1,9},{9,1},{17,25},{25,17},{2,10},{10... | collective-permute-start | bytes 1572872 | tf_op jit(solution)/shard_map/ppermute | solution.py:55
  336.7 32.2 %collective-permute-start.50 = (bf16[128,2048]{1,0:T(8,128)(2,1)}, bf16[128,2048]{1,0:T(8,128)(2,1)S(1)}, u32[]{:S(2)}, u32[]{:S(2)}) collective-permute-start(bf16[128,2048]{1,0:T(8,128)(2,1)} %get-tuple-element.173), channel_id=1, source_target_pairs={{0,16},{8,24},{16,0},{24,8},{1,17},{9,25},{17,1},{25,9},{2,18},{10... | collective-permute-start | bytes 1572872 | tf_op jit(solution)/shard_map/ppermute | solution.py:55
  377.9 39.5 %collective-permute-start.54 = (bf16[512,1024]{1,0:T(8,128)(2,1)S(1)}, bf16[512,1024]{1,0:T(8,128)(2,1)S(1)}, u32[]{:S(2)}, u32[]{:S(2)}) collective-permute-start(bf16[512,1024]{1,0:T(8,128)(2,1)S(1)} %pad_maximum_fusion.13), channel_id=1, source_target_pairs={{0,2},{2,0},{4,6},{6,4},{1,3},{3,1},{5,7},{7,5},{8,10},{10,8},{12,... | collective-permute-start | bytes 3145736 | tf_op jit(solution)/shard_map/ppermute | solution.py:55
  379.1 40.4 %collective-permute-start.70 = (bf16[128,2048]{1,0:T(8,128)(2,1)S(1)}, bf16[128,2048]{1,0:T(8,128)(2,1)S(1)}, u32[]{:S(2)}, u32[]{:S(2)}) collective-permute-start(bf16[128,2048]{1,0:T(8,128)(2,1)S(1)} %bitcast.238), channel_id=1, source_target_pairs={{0,2},{2,0},{4,6},{6,4},{1,3},{3,1},{5,7},{7,5},{8,10},{10,8},{12,... | collective-permute-start | bytes 1572872 | tf_op jit(solution)/shard_map/ppermute | solution.py:55
  381.7 35.6 %collective-permute-start.72 = (bf16[64,2048]{1,0:T(8,128)(2,1)S(1)}, bf16[64,2048]{1,0:T(8,128)(2,1)S(1)}, u32[]{:S(2)}, u32[]{:S(2)}) collective-permute-start(bf16[64,2048]{1,0:T(8,128)(2,1)S(1)} %get-tuple-element.204), channel_id=1, source_target_pairs={{0,4},{2,6},{4,0},{6,2},{1,5},{3,7},{5,1},{7,3},{8,12},{10,14},{12... | collective-permute-start | bytes 786440 | tf_op jit(solution)/shard_map/ppermute | solution.py:55
  384.3 79.7 %collective-permute-start.66 = (bf16[128,1536]{0,1:T(8,128)(2,1)S(1)}, bf16[128,1536]{0,1:T(8,128)(2,1)S(1)}, u32[]{:S(2)}, u32[]{:S(2)}) collective-permute-start(bf16[128,1536]{0,1:T(8,128)(2,1)S(1)} %get-tuple-element.194), channel_id=1, source_target_pairs={{0,16},{8,24},{16,0},{24,8},{1,17},{9,25},{17,1},{25,9},{2,18},{10... | collective-permute-start | bytes 1179656 | tf_op jit(solution)/shard_map/ppermute | solution.py:55
  384.3 79.8 %collective-permute-start.67 = (bf16[128,1536]{0,1:T(8,128)(2,1)S(1)}, bf16[128,1536]{0,1:T(8,128)(2,1)S(1)}, u32[]{:S(2)}, u32[]{:S(2)}) collective-permute-start(bf16[128,1536]{0,1:T(8,128)(2,1)S(1)} %get-tuple-element.196), channel_id=1, source_target_pairs={{0,8},{8,0},{16,24},{24,16},{1,9},{9,1},{17,25},{25,17},{2,10},{10... | collective-permute-start | bytes 1179656 | tf_op jit(solution)/shard_map/ppermute | solution.py:55
  419.7 25.9 %collective-permute-start.71 = (bf16[64,2048]{1,0:T(8,128)(2,1)S(1)}, bf16[64,2048]{1,0:T(8,128)(2,1)S(1)}, u32[]{:S(2)}, u32[]{:S(2)}) collective-permute-start(bf16[64,2048]{1,0:T(8,128)(2,1)S(1)} %add_convert_fusion.31), channel_id=1, source_target_pairs={{0,4},{2,6},{4,0},{6,2},{1,5},{3,7},{5,1},{7,3},{8,12},{10,14},{12... | collective-permute-start | bytes 786440 | tf_op jit(solution)/shard_map/ppermute | solution.py:55
  421.2 34.6 %collective-permute-start.55 = (bf16[256,1024]{1,0:T(8,128)(2,1)S(1)}, bf16[256,1024]{1,0:T(8,128)(2,1)S(1)}, u32[]{:S(2)}, u32[]{:S(2)}) collective-permute-start(bf16[256,1024]{1,0:T(8,128)(2,1)S(1)} %add_convert_fusion.3), channel_id=1, source_target_pairs={{0,4},{2,6},{4,0},{6,2},{1,5},{3,7},{5,1},{7,3},{8,12},{10,14},{12... | collective-permute-start | bytes 1572872 | tf_op jit(solution)/shard_map/ppermute | solution.py:55
  485.5 28.1 %collective-permute-start.56 = (f32[256,1024]{1,0:T(8,128)}, f32[256,1024]{1,0:T(8,128)S(1)}, u32[]{:S(2)}, u32[]{:S(2)}) collective-permute-start(f32[256,1024]{1,0:T(8,128)} %multiply_add_fusion.4), channel_id=1, source_target_pairs={{0,1},{1,0},{2,3},{3,2},{4,5},{5,4},{6,7},{7,6},{8,9},{9,8},{10,11... | collective-permute-start | bytes 3145736 | tf_op jit(solution)/shard_map/ppermute | solution.py:55
  (141 other events, 1436.4 us)
